TPU v7x, 256 devices: a whole 4x4x8 slice. The times are simulated.
256 devices in a mesh: grp: 4 (over y), row: 64 (over z, x, core).
Axes of the slice: x: 4, y: 4, z: 8, core: 2. Of those that a mesh axis runs over, the one named last changes fastest.
Arguments:
- matrix_blocks: bfloat16 [4096, 64, 448], P(('grp', 'row')), may hold values from -0.25 to 0.25
- matrix_columns: int32 [4096, 7], P(('grp', 'row')), may hold values from 0 to 4095, as said below
- prolong_blocks: bfloat16 [4096, 64, 256], P(('grp', 'row')), may hold values from -1.3984375 to 1.3984375
- prolong_columns: int32 [4096, 4], replicated, may hold values from 0 to 511, as said below
Outputs:
- galerkin: bfloat16 [512, 64, 896], P('row')
Inputs may be any that keep to these rules, and one draw needn't show every extreme that they name: `matrix_columns`: slot 0 of row i is i itself; the other slots of a row are distinct fine block rows within [(q - 1) * 16, (q + 2) * 16) modulo 4096, q = i // 16. `prolong_columns`: slot 0 of row j is its own aggregate j // 8; the other slots are distinct coarse blocks within [(q - 1) * 2, (q + 2) * 2) modulo 512, q = j // 16.
All inputs are finite; a program needn't handle non-finite values.
Results may differ from a plain program's by a relative error of at most 0.005.
Values may be sent and summed in bfloat16 or wider, within the bound.
No kernel may reach another device: no remote copies, remote signals or barrier semaphores. Data moves between devices by JAX's collectives and lax.ppermute only.
A program may use at most 64 MiB of HBM per device.

v0:
```python
import jax
import jax.numpy as jnp
from jax import lax
from jax.sharding import PartitionSpec as P

AGS = 8


def shifted(value, axis, by):
    peers = lax.axis_size(axis)
    return lax.ppermute(value, axis, [(i, (i + by) % peers) for i in range(peers)])


def place_onehot(columns, first_column, span_width, modulus):
    relative = jnp.mod(columns - first_column, modulus)
    return relative[..., None] == jnp.arange(span_width, dtype=jnp.int32)


def densify(blocks, columns, first_column, span_width, modulus):
    row_count = blocks.shape[0]
    block_size = blocks.shape[1]
    slot_count = columns.shape[1]
    selector = place_onehot(columns, first_column, span_width, modulus)
    shaped = blocks.reshape(row_count, block_size, slot_count, block_size)
    dense_rows = jnp.zeros((row_count, block_size, span_width, block_size), jnp.bfloat16)
    for slot in range(slot_count):
        chosen = selector[:, None, slot, :, None]
        dense_rows = dense_rows + jnp.where(
            chosen, shaped[:, :, slot, None, :], jnp.zeros((), jnp.bfloat16)
        )
    return dense_rows.reshape(row_count * block_size, span_width * block_size)


def window_products(matrix_rows, local_index, dense_window):
    row_count = matrix_rows.shape[0]
    block_size = matrix_rows.shape[1]
    slots_matrix = local_index.shape[1]
    gathered = jnp.take(dense_window, local_index, axis=0)
    gathered = gathered.reshape(row_count, slots_matrix * block_size, dense_window.shape[2])
    summed = jnp.einsum("rpm,rmn->rpn", matrix_rows, gathered, preferred_element_type=jnp.float32)
    return summed.astype(jnp.bfloat16)


def per_device(matrix_blocks, matrix_columns, prolong_blocks, prolong_columns):
    device_count = lax.axis_size(("grp", "row"))
    device_index = lax.axis_index(("grp", "row"))
    rows_local = matrix_blocks.shape[0]
    block_size = matrix_blocks.shape[1]
    aggregates = rows_local // AGS
    fine_total = device_count * rows_local
    coarse_total = device_count * aggregates
    span_width = 5 * aggregates
    piece_width = span_width * block_size
    window_width = 7 * aggregates * block_size
    previous = shifted(prolong_blocks, ("grp", "row"), 1)
    following = shifted(prolong_blocks, ("grp", "row"), -1)
    halo_blocks = jnp.concatenate([previous, prolong_blocks, following], axis=0)
    halo_first = (device_index - 1) * rows_local
    halo_rows = jnp.mod(halo_first + jnp.arange(3 * rows_local, dtype=jnp.int32), fine_total)
    halo_columns = jnp.take(prolong_columns, halo_rows, axis=0)
    local_index = jnp.mod(matrix_columns - halo_first, fine_total)
    dense_window = densify(
        halo_blocks, halo_columns, (device_index - 2) * aggregates, span_width, coarse_total
    )
    dense_window = dense_window.reshape(3 * rows_local, block_size, piece_width)
    block_turns = rows_local // AGS

    def block_products(inputs):
        return window_products(inputs[0], inputs[1], dense_window)

    products = lax.map(
        block_products,
        (
            matrix_blocks.reshape(block_turns, AGS, block_size, -1),
            local_index.reshape(block_turns, AGS, -1),
        ),
    )
    products = products.reshape(rows_local * block_size, piece_width)
    contract_dims = (((0,), (0,)), ((), ()))

    def widen_piece(piece_rows, offset):
        left_pad = offset * aggregates * block_size
        return jnp.pad(piece_rows, ((0, 0), (left_pad, window_width - piece_width - left_pad)))

    products_previous = shifted(products, ("grp", "row"), 1)
    products_next = shifted(products, ("grp", "row"), -1)
    dense_halo = densify(
        halo_blocks, halo_columns, device_index * aggregates, aggregates, coarse_total
    )
    dense_halo = dense_halo.reshape(3, rows_local * block_size, aggregates * block_size)
    term_previous = lax.dot_general(
        dense_halo[0], products_previous, contract_dims, preferred_element_type=jnp.float32
    )
    term_own = lax.dot_general(
        dense_halo[1], products, contract_dims, preferred_element_type=jnp.float32
    )
    term_next = lax.dot_general(
        dense_halo[2], products_next, contract_dims, preferred_element_type=jnp.float32
    )
    accumulated = (
        widen_piece(term_previous, 0) + widen_piece(term_own, 1) + widen_piece(term_next, 2)
    )
    owned_rows = accumulated.astype(jnp.bfloat16).reshape(aggregates, block_size, window_width)
    return lax.all_gather(owned_rows, "grp", axis=0, tiled=True)


def solution(mesh):
    placed = (
        P(("grp", "row"), None, None),
        P(("grp", "row"), None),
        P(("grp", "row"), None, None),
        P(),
    )
    return jax.shard_map(
        per_device, mesh=mesh, in_specs=placed, out_specs=P("row", None, None), check_vma=False
    )
```

profile of v0, /device:TPU:0, one launch (start us, length us, event | category | flops | bytes accessed | tf_op | source)
XLA Modules:
  0.0 183.9 jit_solution(5731913888417775049)
XLA Ops:
  0.0 8.2 %collective-permute-start.1 = (bf16[16,64,256]{2,1,0:T(8,128)(2,1)}, bf16[16,64,256]{2,1,0:T(8,128)(2,1)}, u32[]{:S(2)}, u32[]{:S(2)}) collective-permute-start(bf16[16,64,256]{2,1,0:T(8,128)(2,1)} %param.8), channel_id=1, source_target_pairs={{0,255},{1,0},{2,1},{3,2},{4,3},{5,4},{6,5},{7,6},{8,7},{9,8},{10,... | collective-permute-start | bytes 1572872 | tf_op jit(solution)/shard_map/ppermute | solution.py:11
  8.2 0.7 add_select_fusion.2
  9.0 1.5 copy.47
  10.5 0.6 gather_fusion.1
  12.0 0.2 broadcast_in_dim.229
  12.2 0.2 broadcast_in_dim.230
  12.5 0.2 broadcast_in_dim.224
  12.7 0.2 broadcast_in_dim.217
  12.9 0.2 broadcast_in_dim.218
  13.1 0.2 broadcast_in_dim.210
  13.3 0.2 broadcast_in_dim.211
  13.5 1.8 collective-permute-done
  15.3 2.4 %pad_maximum_fusion = bf16[48,64,256]{2,1,0:T(8,128)(2,1)} fusion(bf16[16,64,256]{2,1,0:T(8,128)(2,1)} %collective-permute-done.1, bf16[16,64,256]{2,1,0:T(8,128)(2,1)S(1)} %copy-done.5, bf16[16,64,256]{2,1,0:T(8,128)(2,1)S(1)} %collective-permute-done), kind=kLoop, calls=%fused_computation.29 | loop fusion | flops 1572864 | bytes 3145728 | tf_op jit(solution)/shard_map/concatenate | solution.py:57
  17.7 4.6 %reshape.184 = bf16[48,64,4,64]{3,2,1,0:T(4,128)(2,1)S(1)} reshape(bf16[48,64,256]{2,1,0:T(8,128)(2,1)} %pad_maximum_fusion) | data formatting | bytes 3145728 | tf_op jit(solution)/shard_map/reshape | solution.py:24
  22.3 8.2 %fusion.19 = (bf16[48,64,1,64]{3,2,1,0:T(2,128)(2,1)}, bf16[48,64,1,64]{3,2,1,0:T(2,128)(2,1)}, bf16[48,64,1,64]{3,2,1,0:T(2,128)(2,1)}, bf16[48,64,1,64]{3,2,1,0:T(2,128)(2,1)}) fusion(bf16[48,64,4,64]{3,2,1,0:T(4,128)(2,1)S(1)} %reshape.184), kind=kLoop, calls=%fused_computation.70 | loop fusion | bytes 3145728 | tf_op jit(solution)/shard_map/slice | solution.py:29
  30.4 3.8 %copy.64 = bf16[48,64,1,64]{1,3,0,2:T(8,128)(2,1)S(1)} copy(bf16[48,64,1,64]{3,2,1,0:T(2,128)(2,1)} %get-tuple-element.141) | data formatting | bytes 786432
  34.2 2.9 %copy_bitcast_fusion.2 = (bf16[48,64,64]{2,1,0:T(8,128)(2,1)}, bf16[48,64,64]{2,1,0:T(8,128)(2,1)}) fusion(bf16[48,64,1,64]{3,2,1,0:T(2,128)(2,1)S(1)} %copy-done, bf16[48,64,1,64]{3,2,1,0:T(2,128)(2,1)} %get-tuple-element.141), kind=kLoop, calls=%fused_computation.32 | loop fusion | bytes 1572864
  37.1 1.8 %copy.65 = bf16[48,64,1,64]{1,3,0,2:T(8,128)(2,1)S(1)} copy(bf16[48,64,1,64]{3,2,1,0:T(2,128)(2,1)S(1)} %copy-done) | data formatting | bytes 786432
  38.9 3.7 %copy.67 = bf16[48,64,1,64]{1,3,0,2:T(8,128)(2,1)S(1)} copy(bf16[48,64,1,64]{3,2,1,0:T(2,128)(2,1)} %get-tuple-element.142) | data formatting | bytes 786432
  42.6 3.4 %copy_bitcast_fusion = (bf16[48,64,64]{2,1,0:T(8,128)(2,1)}, bf16[48,64,64]{2,1,0:T(8,128)(2,1)}) fusion(bf16[48,64,1,64]{3,2,1,0:T(2,128)(2,1)} %get-tuple-element.142, bf16[48,64,1,64]{3,2,1,0:T(2,128)(2,1)} %get-tuple-element.143), kind=kLoop, calls=%fused_computation.30 | loop fusion | bytes 1572864
  46.0 3.6 %copy.66 = bf16[48,64,1,64]{1,3,0,2:T(8,128)(2,1)S(1)} copy(bf16[48,64,1,64]{3,2,1,0:T(2,128)(2,1)} %get-tuple-element.143) | data formatting | bytes 786432
  49.6 87.8 %while.11 = (s32[]{:T(128)}, bf16[2,8,64,640]{3,2,1,0:T(8,128)(2,1)}, bf16[2,8,64,448]{3,2,1,0:T(8,128)(2,1)}, s32[2,8,7]{2,1,0:T(8,128)S(1)}, bf16[48,64,64]{1,...) while((s32[]{:T(128)}, ...), condition=%wide.region_1.2_spmd.clone, body=%wide.region_0.1_spmd.clone.sunk | while | flops 309986816 | bytes 53098444 | solution.py:71
  50.1 19.1 %fusion.37 = bf16[48,64,640]{1,2,0:T(8,128)(2,1)} fusion(pred[48,640]{1,0:T(8,128)(4,1)S(1)} %get-tuple-element.276, pred[48,640]{1,0:T(8,128)(4,1)S(1)} %get-tuple-element.274, pred[48,640]{1,0:T(8,128)(4,1)S(1)} %get-tuple-element.272, pred[48,640]{1,0:T(8,128)(4,1)S(1)} %get-tuple-element.270, bf16[48,64,64]{1,2,0:T(8,128)(2,1)S(1)} %get-tuple-element.275, ...), kind=kLoop, calls=%fused_computation.4.clone.1 | loop fusion | flops 13762560 | bytes 5627904 | tf_op jit(solution)/shard_map/add | solution.py:28
  69.2 9.3 %gather_fusion = bf16[56,64,640]{1,2,0:T(8,128)(2,1)} fusion(bf16[48,64,640]{1,2,0:T(8,128)(2,1)} %fusion.37, s32[1024]{0:T(1024)S(1)} %pad_clamp_fusion.3), kind=kCustom, calls=%fused_computation.clone.clone.1 | custom fusion | bytes 9175264 | tf_op jit(solution)/shard_map/while/body/eval_jaxpr/jit(_take)/gather | solution.py:38
  78.6 9.9 %copy.77 = bf16[56,64,640]{2,1,0:T(8,128)(2,1)} copy(bf16[56,64,640]{1,2,0:T(8,128)(2,1)} %gather_fusion) | data formatting | bytes 9175040 | tf_op jit(solution)/shard_map/while/body/eval_jaxpr/jit(_take)/gather | solution.py:38
  88.5 3.0 %bitcast_select_fusion.6 = bf16[8,448,640]{2,1,0:T(8,128)(2,1)S(1)} fusion(pred[8,448]{1,0:T(8,128)(4,1)S(1)} %broadcast_in_dim.352, bf16[8,448,640]{2,1,0:T(8,128)(2,1)} %bitcast.99), kind=kLoop, calls=%fused_computation.10.clone.1 | loop fusion | flops 2293760 | bytes 9178624 | tf_op jit(solution)/shard_map/while/body/eval_jaxpr/jit(_take)/select_n | solution.py:38
  91.5 0.9 fusion.38
  92.5 1.1 copy-done.3
  94.0 19.1 %fusion.37 = bf16[48,64,640]{1,2,0:T(8,128)(2,1)} fusion(pred[48,640]{1,0:T(8,128)(4,1)S(1)} %get-tuple-element.276, pred[48,640]{1,0:T(8,128)(4,1)S(1)} %get-tuple-element.274, pred[48,640]{1,0:T(8,128)(4,1)S(1)} %get-tuple-element.272, pred[48,640]{1,0:T(8,128)(4,1)S(1)} %get-tuple-element.270, bf16[48,64,64]{1,2,0:T(8,128)(2,1)S(1)} %get-tuple-element.275, ...), kind=kLoop, calls=%fused_computation.4.clone.1 | loop fusion | flops 13762560 | bytes 5627904 | tf_op jit(solution)/shard_map/add | solution.py:28
  113.1 9.3 %gather_fusion = bf16[56,64,640]{1,2,0:T(8,128)(2,1)} fusion(bf16[48,64,640]{1,2,0:T(8,128)(2,1)} %fusion.37, s32[1024]{0:T(1024)S(1)} %pad_clamp_fusion.3), kind=kCustom, calls=%fused_computation.clone.clone.1 | custom fusion | bytes 9175264 | tf_op jit(solution)/shard_map/while/body/eval_jaxpr/jit(_take)/gather | solution.py:38
  122.5 9.9 %copy.77 = bf16[56,64,640]{2,1,0:T(8,128)(2,1)} copy(bf16[56,64,640]{1,2,0:T(8,128)(2,1)} %gather_fusion) | data formatting | bytes 9175040 | tf_op jit(solution)/shard_map/while/body/eval_jaxpr/jit(_take)/gather | solution.py:38
  132.4 3.0 %bitcast_select_fusion.6 = bf16[8,448,640]{2,1,0:T(8,128)(2,1)S(1)} fusion(pred[8,448]{1,0:T(8,128)(4,1)S(1)} %broadcast_in_dim.352, bf16[8,448,640]{2,1,0:T(8,128)(2,1)} %bitcast.99), kind=kLoop, calls=%fused_computation.10.clone.1 | loop fusion | flops 2293760 | bytes 9178624 | tf_op jit(solution)/shard_map/while/body/eval_jaxpr/jit(_take)/select_n | solution.py:38
  135.4 0.9 fusion.38
  136.3 1.1 copy-done.3
  137.4 7.3 %collective-permute-start.3 = (bf16[1024,640]{1,0:T(8,128)(2,1)}, bf16[1024,640]{1,0:T(8,128)(2,1)}, u32[]{:S(2)}, u32[]{:S(2)}) collective-permute-start(bf16[1024,640]{1,0:T(8,128)(2,1)} %bitcast.105), channel_id=1, source_target_pairs={{0,255},{1,0},{2,1},{3,2},{4,3},{5,4},{6,5},{7,6},{8,7},{9,8},{10,... | collective-permute-start | bytes 3932168 | tf_op jit(solution)/shard_map/ppermute | solution.py:11
  144.7 6.6 %fusion.12 = bf16[48,64,2,64]{3,2,1,0:T(2,128)(2,1)S(1)} fusion(pred[48,2]{1,0:T(8,128)(4,1)S(1)} %copy.49, pred[48,2]{1,0:T(8,128)(4,1)S(1)} %copy.50, pred[48,2]{1,0:T(8,128)(4,1)S(1)} %copy.51, pred[48,2]{1,0:T(8,128)(4,1)S(1)} %copy.52, bf16[48,64,64]{2,1,0:T(8,128)(2,1)} %get-tuple-element.158, bf16[48,64,64]{2,1,0:T(8,128)(2,1)} %get-tuple-element.159, ...), kind=kLoop, calls=%fused_computation.28 | loop fusion | flops 2752512 | bytes 2359680 | tf_op jit(solution)/shard_map/add | solution.py:28
  151.3 1.3 fusion.20
  152.6 0.2 squeeze.19
  152.8 0.2 squeeze.21
  153.1 0.2 squeeze.20
  153.4 0.5 copy-done.4
  153.9 0.4 fusion.22
  154.3 5.8 %collective-permute-done.3 = bf16[1024,640]{1,0:T(8,128)(2,1)} collective-permute-done((bf16[1024,640]{1,0:T(8,128)(2,1)}, bf16[1024,640]{1,0:T(8,128)(2,1)}, u32[]{:S(2)}, u32[]{:S(2)}) %collective-permute-start.3) | collective-permute-done | bytes 1310752 | tf_op jit(solution)/shard_map/ppermute | solution.py:11
  160.1 1.7 fusion.23
  161.9 5.7 %collective-permute-done.2 = bf16[1024,640]{1,0:T(8,128)(2,1)} collective-permute-done((bf16[1024,640]{1,0:T(8,128)(2,1)}, bf16[1024,640]{1,0:T(8,128)(2,1)}, u32[]{:S(2)}, u32[]{:S(2)}) %collective-permute-start.2) | collective-permute-done | bytes 1310752 | tf_op jit(solution)/shard_map/ppermute | solution.py:11
  167.6 1.7 fusion.21
  169.4 13.6 %all_gather.3 = bf16[8,64,896]{2,1,0:T(8,128)(2,1)S(1)} all-gather(bf16[2,64,896]{2,1,0:T(8,128)(2,1)S(1)} %bitcast.108), channel_id=1, replica_groups=mesh['grp'=4,'row'=64] {'grp'}, dimensions={0}, use_global_device_ids=true | all-gather | bytes 1146880 | tf_op jit(solution)/shard_map/all_gather | solution.py:104
  182.9 0.9 copy.88
  (52 shorter events, 2.1 us)
Async XLA Ops:
  0.0 15.3 %collective-permute-start = (bf16[16,64,256]{2,1,0:T(8,128)(2,1)}, bf16[16,64,256]{2,1,0:T(8,128)(2,1)S(1)}, u32[]{:S(2)}, u32[]{:S(2)}) collective-permute-start(bf16[16,64,256]{2,1,0:T(8,128)(2,1)} %param.8), channel_id=1, source_target_pairs={{0,1},{1,2},{2,3},{3,4},{4,5},{5,6},{6,7},{7,8},{8,9},{9,10},{10,1... | collective-permute-start | bytes 1572872 | tf_op jit(solution)/shard_map/ppermute | solution.py:11
  0.0 15.3 %collective-permute-start.1 = (bf16[16,64,256]{2,1,0:T(8,128)(2,1)}, bf16[16,64,256]{2,1,0:T(8,128)(2,1)}, u32[]{:S(2)}, u32[]{:S(2)}) collective-permute-start(bf16[16,64,256]{2,1,0:T(8,128)(2,1)} %param.8), channel_id=1, source_target_pairs={{0,255},{1,0},{2,1},{3,2},{4,3},{5,4},{6,5},{7,6},{8,7},{9,8},{10,... | collective-permute-start | bytes 1572872 | tf_op jit(solution)/shard_map/ppermute | solution.py:11
  9.0 6.3 %copy-start.5 = (bf16[16,64,256]{2,1,0:T(8,128)(2,1)S(1)}, bf16[16,64,256]{2,1,0:T(8,128)(2,1)}, u32[]{:S(2)}) copy-start(bf16[16,64,256]{2,1,0:T(8,128)(2,1)} %param.8) | copy-start | bytes 1572868
  30.4 3.8 %copy-start = (bf16[48,64,1,64]{3,2,1,0:T(2,128)(2,1)S(1)}, bf16[48,64,1,64]{3,2,1,0:T(2,128)(2,1)}, u32[]{:S(2)}) copy-start(bf16[48,64,1,64]{3,2,1,0:T(2,128)(2,1)} %get-tuple-element.144) | copy-start | bytes 1179652
  88.5 3.0 %copy-start.1 = (bf16[2,8,64,448]{3,2,1,0:T(8,128)(2,1)S(1)}, bf16[2,8,64,448]{3,2,1,0:T(8,128)(2,1)}, u32[]{:S(2)}) copy-start(bf16[2,8,64,448]{3,2,1,0:T(8,128)(2,1)} %get-tuple-element.267) | copy-start | bytes 2752516 | tf_op jit(solution)/shard_map/while
  88.5 3.0 %copy-start.2 = (bf16[2,8,64,640]{3,2,1,0:T(8,128)(2,1)S(1)}, bf16[2,8,64,640]{3,2,1,0:T(8,128)(2,1)}, u32[]{:S(2)}) copy-start(bf16[2,8,64,640]{3,2,1,0:T(8,128)(2,1)} %get-tuple-element.253) | copy-start | bytes 3932164 | tf_op jit(solution)/shard_map/while
  92.4 1.1 copy-start.3
  132.4 3.0 %copy-start.1 = (bf16[2,8,64,448]{3,2,1,0:T(8,128)(2,1)S(1)}, bf16[2,8,64,448]{3,2,1,0:T(8,128)(2,1)}, u32[]{:S(2)}) copy-start(bf16[2,8,64,448]{3,2,1,0:T(8,128)(2,1)} %get-tuple-element.267) | copy-start | bytes 2752516 | tf_op jit(solution)/shard_map/while
  132.4 3.0 %copy-start.2 = (bf16[2,8,64,640]{3,2,1,0:T(8,128)(2,1)S(1)}, bf16[2,8,64,640]{3,2,1,0:T(8,128)(2,1)}, u32[]{:S(2)}) copy-start(bf16[2,8,64,640]{3,2,1,0:T(8,128)(2,1)} %get-tuple-element.253) | copy-start | bytes 3932164 | tf_op jit(solution)/shard_map/while
  136.3 1.1 copy-start.3
  137.4 22.7 %collective-permute-start.3 = (bf16[1024,640]{1,0:T(8,128)(2,1)}, bf16[1024,640]{1,0:T(8,128)(2,1)}, u32[]{:S(2)}, u32[]{:S(2)}) collective-permute-start(bf16[1024,640]{1,0:T(8,128)(2,1)} %bitcast.105), channel_id=1, source_target_pairs={{0,255},{1,0},{2,1},{3,2},{4,3},{5,4},{6,5},{7,6},{8,7},{9,8},{10,... | collective-permute-start | bytes 3932168 | tf_op jit(solution)/shard_map/ppermute | solution.py:11
  144.7 22.9 %collective-permute-start.2 = (bf16[1024,640]{1,0:T(8,128)(2,1)}, bf16[1024,640]{1,0:T(8,128)(2,1)}, u32[]{:S(2)}, u32[]{:S(2)}) collective-permute-start(bf16[1024,640]{1,0:T(8,128)(2,1)} %bitcast.106), channel_id=1, source_target_pairs={{0,1},{1,2},{2,3},{3,4},{4,5},{5,6},{6,7},{7,8},{8,9},{9,10},{10,1... | collective-permute-start | bytes 3932168 | tf_op jit(solution)/shard_map/ppermute | solution.py:11
  152.6 1.3 copy-start.4
where the time goes:
time: 185 us; the launch traced here: 184 us
  local copies, waits for them, and re-layouts  81.2 us (44%)
  other arithmetic  54.2 us (29%)
  starting transfers between devices  15.5 us (8%)
  blocking collectives  13.6 us (7%)
  waiting for transfers between devices  13.4 us (7%)
  matrix products  5.69 us (3%)
    add x3, other arithmetic, densify(): dense_rows + jnp.where(chosen, shaped[:, :, slot, None, :], jnp.zeros((),...  44.8 us
    gather x4, local copies, waits for them, and re-layouts, window_products(): gathered = jnp.take(dense_window, local_index, axis=0)  38.5 us
    unnamed x15, local copies, waits for them, and re-layouts  22.3 us
    ppermute x4, starting transfers between devices, shifted(): lax.ppermute(value, axis, [(i, (i + by) % peers) for i in range(peers)])  15.5 us
    all_gather x1, blocking collectives, per_device(): return lax.all_gather(owned_rows, 'grp', axis=0, tiled=True)  13.6 us
    ppermute x4, waiting for transfers between devices, shifted(): lax.ppermute(value, axis, [(i, (i + by) % peers) for i in range(peers)])  13.4 us
    slice x1, local copies, waits for them, and re-layouts, densify(): shaped[:, :, slot, None, :]  8.15 us
    select_n x4, other arithmetic, window_products(): gathered = jnp.take(dense_window, local_index, axis=0)  6 us
  transfers between devices with their start and end apart: 4, of which 3 were waited for; matrix products, arithmetic and copies ran while one was open for 9% of the time, Pallas kernels for 0%

commit v1 on v0

v1 whole, which is shorter than its diff:
```python
import jax
import jax.numpy as jnp
from jax import lax
from jax.experimental import pallas as pl
from jax.experimental.pallas import tpu as pltpu
from jax.sharding import PartitionSpec as P

AGS = 8
BS = 64
LANES = 128
VMEM_BYTES = 48 * 1024 * 1024


def shifted(value, axis, by):
    peers = lax.axis_size(axis)
    return lax.ppermute(value, axis, [(i, (i + by) % peers) for i in range(peers)])


def spread(blocks_ref, columns_ref, dense_ref):
    rows, _, width = blocks_ref.shape
    low = lax.broadcasted_iota(jnp.int32, (BS, LANES), 1) < BS
    for row in range(rows):
        for slot in range(width // BS):
            block = blocks_ref[row, :, slot * BS : (slot + 1) * BS]
            both = jnp.concatenate([block, block], axis=1)
            column = columns_ref[slot, row]
            place = dense_ref.at[column // 2, row * BS : (row + 1) * BS, :]
            place[...] = jnp.where(low == (column % 2 == 0), both, place[...])


def left_kernel(a_cols_ref, p_cols_ref, a_ref, p_ref, left_ref, own_ref, dense_a_ref, dense_p_ref):
    dense_a_ref[...] = jnp.zeros_like(dense_a_ref)
    dense_p_ref[...] = jnp.zeros_like(dense_p_ref)
    spread(p_ref, p_cols_ref, dense_p_ref)
    spread(a_ref, a_cols_ref, dense_a_ref)
    tiles = dense_p_ref.shape[0]
    p_dense = jnp.concatenate([dense_p_ref[t] for t in range(tiles)], axis=1)
    p_turned = p_dense.T
    groups = left_ref.shape[0]
    per_group = dense_a_ref.shape[0] // groups
    for group in range(groups):
        a_dense = jnp.concatenate(
            [dense_a_ref[group * per_group + t] for t in range(per_group)], axis=1
        )
        part = jnp.dot(p_turned, a_dense, preferred_element_type=jnp.float32)
        left_ref[group] = part.astype(jnp.bfloat16)
    own_ref[...] = jnp.dot(left_ref[1], p_dense, preferred_element_type=jnp.float32)


def right_kernel(
    before_cols_ref, after_cols_ref, before_ref, after_ref, left_ref, own_ref,
    to_before_ref, stay_ref, to_after_ref, dense_before_ref, dense_after_ref,
):
    dense_before_ref[...] = jnp.zeros_like(dense_before_ref)
    dense_after_ref[...] = jnp.zeros_like(dense_after_ref)
    spread(before_ref, before_cols_ref, dense_before_ref)
    spread(after_ref, after_cols_ref, dense_after_ref)

    def term(group, dense_ref):
        dense = jnp.concatenate([dense_ref[t] for t in range(dense_ref.shape[0])], axis=1)
        return jnp.dot(left_ref[group], dense, preferred_element_type=jnp.float32)

    before = term(0, dense_before_ref)
    after = term(2, dense_after_ref)
    own = own_ref[...]
    step = LANES
    summed = jnp.concatenate(
        [
            before[:, :step],
            before[:, step : 2 * step] + own[:, :step],
            before[:, 2 * step :] + own[:, step : 2 * step] + after[:, :step],
            own[:, 2 * step :] + after[:, step : 2 * step],
            after[:, 2 * step :],
        ],
        axis=1,
    )
    rows = stay_ref.shape[0]
    to_before_ref[...] = summed[:rows].astype(to_before_ref.dtype)
    stay_ref[...] = summed[rows : 2 * rows]
    to_after_ref[...] = summed[2 * rows :].astype(to_after_ref.dtype)


def per_device(matrix_blocks, matrix_columns, prolong_blocks, prolong_columns):
    both = ("grp", "row")
    device_count = lax.axis_size(both)
    device_index = lax.axis_index(both)
    rows = matrix_blocks.shape[0]
    aggregates = rows // AGS
    fine_total = device_count * rows
    coarse_total = device_count * aggregates
    side = aggregates * BS
    before_blocks = shifted(prolong_blocks, both, 1)
    after_blocks = shifted(prolong_blocks, both, -1)

    a_cols = jnp.mod(matrix_columns.T - (device_index - 1) * rows, fine_total)
    columns_turned = prolong_columns.T

    def group_cols(offset):
        group = jnp.mod(device_index + offset, device_count)
        cols = lax.dynamic_slice_in_dim(columns_turned, group * rows, rows, 1)
        return jnp.mod(cols - (group - 1) * aggregates, coarse_total)

    bf16 = jnp.bfloat16
    f32 = jnp.float32
    smem = pl.BlockSpec(memory_space=pltpu.SMEM)
    vmem = pl.BlockSpec(memory_space=pltpu.VMEM)
    params = pltpu.CompilerParams(vmem_limit_bytes=VMEM_BYTES)
    left, own = pl.pallas_call(
        left_kernel,
        out_shape=(
            jax.ShapeDtypeStruct((3, 3 * side, rows * BS), bf16),
            jax.ShapeDtypeStruct((3 * side, 3 * side), f32),
        ),
        in_specs=[smem, smem, vmem, vmem],
        out_specs=(vmem, vmem),
        scratch_shapes=[
            pltpu.VMEM((3 * rows * BS // LANES, rows * BS, LANES), bf16),
            pltpu.VMEM((3 * side // LANES, rows * BS, LANES), bf16),
        ],
        compiler_params=params,
        name="left_kernel",
    )(a_cols, group_cols(0), matrix_blocks, prolong_blocks)

    dense = pltpu.VMEM((3 * side // LANES, rows * BS, LANES), bf16)
    to_before, stay, to_after = pl.pallas_call(
        right_kernel,
        out_shape=(
            jax.ShapeDtypeStruct((side, 5 * side), bf16),
            jax.ShapeDtypeStruct((side, 5 * side), f32),
            jax.ShapeDtypeStruct((side, 5 * side), bf16),
        ),
        in_specs=[smem, smem, vmem, vmem, vmem, vmem],
        out_specs=(vmem, vmem, vmem),
        scratch_shapes=[dense, dense],
        compiler_params=params,
        name="right_kernel",
    )(group_cols(-1), group_cols(1), before_blocks, after_blocks, left, own)

    from_before = shifted(to_after, both, 1)
    from_after = shifted(to_before, both, -1)

    def widen(part, offset):
        return jnp.pad(part.astype(f32), ((0, 0), (offset * side, (2 - offset) * side)))

    total = widen(from_before, 0) + widen(stay, 1) + widen(from_after, 2)
    owned = total.astype(bf16).reshape(aggregates, BS, 7 * side)
    return lax.all_gather(owned, "grp", axis=0, tiled=True)


def solution(mesh):
    placed = (
        P(("grp", "row"), None, None),
        P(("grp", "row"), None),
        P(("grp", "row"), None, None),
        P(),
    )
    return jax.shard_map(
        per_device, mesh=mesh, in_specs=placed, out_specs=P("row", None, None), check_vma=False
    )
```

time: 185 us -> 45.5 us (0.25)
  local copies, waits for them, and re-layouts: 81.2 us -> 3.19 us
  other arithmetic: 54.2 us -> 1.59 us
  waiting for transfers between devices: 13.4 us -> 3.11 us
  Pallas kernels: 0 us -> 8.27 us
  matrix products: 5.69 us -> 0 us
    add x3 -> x0, other arithmetic: 44.8 us -> none  [densify(): dense_rows + jnp.where(chosen, shaped[:, :, slot, None, :], jnp.zeros((),...]
    gather x5 -> x0, local copies, waits for them, and re-layouts: 39.1 us -> none  [the longest x4 38.5 us: window_products(): gathered = jnp.take(dense_window, local_index, axis=0)]
    unnamed x15 -> x5, local copies, waits for them, and re-layouts: 22.3 us -> 3.19 us
    ppermute x4, waiting for transfers between devices: 13.4 us -> 3.11 us  [shifted(): lax.ppermute(value, axis, [(i, (i + by) % peers) for i in range(peers)])]
    slice x2 -> x0, local copies, waits for them, and re-layouts: 9.47 us -> none  [the longest x1 8.15 us: densify(): shaped[:, :, slot, None, :]]
    pallas_call x0 -> x2, Pallas kernels: none -> 8.27 us  [the longest x1 5.82 us: per_device(): pl.pallas_call(left_kernel, out_shape=(jax.ShapeDtypeStruct((3, 3 * side,...]
    dot_general x5 -> x0, matrix products: 5.69 us -> none  [the longest x2 1.85 us: window_products(): jnp.einsum('rpm,rmn->rpn', matrix_rows, gathered, preferred_element_type=...]
    select_n x7 -> x2, other arithmetic: 6.8 us -> 1.53 us  [the longest x1 0.84 us: group_cols(): return jnp.mod(cols - (group - 1) * aggregates, coarse_total)]
  transfers between devices with their start and end apart: 4 -> 4, of which waited for: 3 -> 1; matrix products, arithmetic and copies ran while one was open for 9% -> 3% of each run, Pallas kernels for 0% -> 13%
where the time goes in v1:
time: 45.5 us; the launch traced here: 45.2 us
  starting transfers between devices  15.5 us (34%)
  blocking collectives  13.6 us (30%)
  Pallas kernels  8.27 us (18%)
  local copies, waits for them, and re-layouts  3.19 us (7%)
  waiting for transfers between devices  3.11 us (7%)
  other arithmetic  1.59 us (3%)
    ppermute x4, starting transfers between devices, shifted(): lax.ppermute(value, axis, [(i, (i + by) % peers) for i in range(peers)])  15.5 us
    all_gather x1, blocking collectives, per_device(): return lax.all_gather(owned, 'grp', axis=0, tiled=True)  13.6 us
    pallas_call x1, Pallas kernels, per_device(): pl.pallas_call(left_kernel, out_shape=(jax.ShapeDtypeStruct((3, 3 * side,...  5.82 us
    unnamed x5, local copies, waits for them, and re-layouts  3.19 us
    ppermute x4, waiting for transfers between devices, shifted(): lax.ppermute(value, axis, [(i, (i + by) % peers) for i in range(peers)])  3.11 us
    pallas_call x1, Pallas kernels, per_device(): pl.pallas_call(right_kernel, out_shape=(jax.ShapeDtypeStruct((side, 5 * s...  2.45 us
  transfers between devices with their start and end apart: 4, of which 1 were waited for; matrix products, arithmetic and copies ran while one was open for 3% of the time, Pallas kernels for 13%

profile of v1, /device:TPU:0, one launch (start us, length us, event | category | flops | bytes accessed | tf_op | source)
XLA Modules:
  0.0 45.2 jit_solution(7266575828787653913)
XLA Ops:
  0.0 0.0 collective-permute-start
  0.0 8.2 %collective-permute-start.1 = (bf16[16,64,256]{2,1,0:T(8,128)(2,1)}, bf16[16,64,256]{2,1,0:T(8,128)(2,1)S(1)}, u32[]{:S(2)}, u32[]{:S(2)}) collective-permute-start(bf16[16,64,256]{2,1,0:T(8,128)(2,1)} %p_ref.1), channel_id=1, source_target_pairs={{0,255},{1,0},{2,1},{3,2},{4,3},{5,4},{6,5},{7,6},{8,7},{9,8},{10,... | collective-permute-start | bytes 1572872 | tf_op jit(solution)/shard_map/ppermute | solution.py:16
  8.2 0.8 %add_select_fusion.1 = (s32[4,16]{1,0:T(4,128)S(1)}, s32[4,16]{1,0:T(4,128)S(1)}, s32[4,16]{1,0:T(4,128)S(1)}) fusion(s32[4096,4]{0,1:T(4,128)} %param.7, s32[]{:T(128)S(6)} %select_n.52, s32[]{:T(128)S(6)} %mul.31, s32[]{:T(128)S(6)} %mul.26, s32[]{:T(128)S(6)} %select_n.45, s32[]{:T(128)S(6)} %mul.28, s32[]{:T(128)S(6)} %select_n.48), kind=kLoop, calls=%fused_computation.5 | loop fusion | flops 2304 | bytes 1560 | tf_op jit(solution)/shard_map/jit(remainder)/select_n | solution.py:101
  9.0 0.7 %add_select_fusion.a_cols_ref = s32[7,16]{1,0:T(8,128)S(1)} fusion(s32[16,7]{0,1:T(8,128)} %param.5, s32[]{:T(128)S(6)} %mul.29), kind=kLoop, calls=%fused_computation.1 | loop fusion | flops 1344 | bytes 900 | tf_op jit(solution)/shard_map/jit(remainder)/select_n | solution.py:95
  9.7 0.0 copy-start
  9.7 1.2 %copy-done = bf16[16,64,448]{2,1,0:T(8,128)(2,1)S(1)} copy-done((bf16[16,64,448]{2,1,0:T(8,128)(2,1)S(1)}, bf16[16,64,448]{2,1,0:T(8,128)(2,1)}, u32[]{:S(2)}) %copy-start) | copy-done | bytes 917528
  11.0 0.0 copy-start.1
  11.0 1.0 %copy-done.1 = bf16[16,64,256]{2,1,0:T(8,128)(2,1)S(1)} copy-done((bf16[16,64,256]{2,1,0:T(8,128)(2,1)S(1)}, bf16[16,64,256]{2,1,0:T(8,128)(2,1)}, u32[]{:S(2)}) %copy-start.1) | copy-done | bytes 524312
  12.0 5.8 %left_kernel.1 = (bf16[3,384,1024]{2,1,0:T(8,128)(2,1)S(1)}, f32[384,384]{1,0:T(8,128)S(1)}) custom-call(s32[7,16]{1,0:T(8,128)S(1)} %add_select_fusion.a_cols_ref, s32[4,16]{1,0:T(4,128)S(1)} %get-tuple-element.15.p_cols_ref, bf16[16,64,448]{2,1,0:T(8,128)(2,1)S(1)} %copy-done, bf16[16,64,256]{2,1,0:T(8,128)(2,1)S(1)} %copy-done.1), custom_call_target="tpu_custom_call" | custom-call | tf_op jit(solution)/shard_map/left_kernel/pallas_call | solution.py:108
  17.8 0.0 collective-permute-done.before_ref
  17.9 0.0 collective-permute-done.1.after_ref
  17.9 2.4 %right_kernel.1 = (bf16[128,640]{1,0:T(8,128)(2,1)S(1)}, f32[128,640]{1,0:T(8,128)S(1)}, bf16[128,640]{1,0:T(8,128)(2,1)S(1)}) custom-call(s32[4,16]{1,0:T(4,128)S(1)} %get-tuple-element.16.before_cols_ref, s32[4,16]{1,0:T(4,128)S(1)} %get-tuple-element.17.after_cols_ref, bf16[16,64,256]{2,1,0:T(8,128)(2,1)S(1)} %collective-permute-done.before_ref, ...), custom_call_target="tpu_custom_call" | custom-call | tf_op jit(solution)/shard_map/right_kernel/pallas_call | solution.py:125
  20.3 0.1 collective-permute-start.2
  20.4 7.2 %collective-permute-start.3 = (bf16[128,640]{1,0:T(8,128)(2,1)S(1)}, bf16[128,640]{1,0:T(8,128)(2,1)S(1)}, u32[]{:S(2)}, u32[]{:S(2)}) collective-permute-start(bf16[128,640]{1,0:T(8,128)(2,1)S(1)} %get-tuple-element.14), channel_id=1, source_target_pairs={{0,255},{1,0},{2,1},{3,2},{4,3},{5,4},{6,5},{7,6},{8,7},{9,8},{10,... | collective-permute-start | bytes 491528 | tf_op jit(solution)/shard_map/ppermute | solution.py:16
  27.6 3.1 %collective-permute-done.2 = bf16[128,640]{1,0:T(8,128)(2,1)S(1)} collective-permute-done((bf16[128,640]{1,0:T(8,128)(2,1)S(1)}, bf16[128,640]{1,0:T(8,128)(2,1)S(1)}, u32[]{:S(2)}, u32[]{:S(2)}) %collective-permute-start.2) | collective-permute-done | bytes 163872 | tf_op jit(solution)/shard_map/ppermute | solution.py:16
  30.7 0.0 collective-permute-done.3
  30.7 0.1 add_convert_fusion
  30.7 13.6 %all_gather.3 = bf16[8,64,896]{2,1,0:T(8,128)(2,1)S(1)} all-gather(bf16[2,64,896]{2,1,0:T(8,128)(2,1)S(1)} %bitcast.17), channel_id=1, replica_groups=mesh['grp'=4,'row'=64] {'grp'}, dimensions={0}, use_global_device_ids=true | all-gather | bytes 1146880 | tf_op jit(solution)/shard_map/all_gather | solution.py:147
  44.3 0.9 %copy.6 = bf16[8,64,896]{2,1,0:T(8,128)(2,1)} copy(bf16[8,64,896]{2,1,0:T(8,128)(2,1)S(1)} %all_gather.3) | data formatting | bytes 1835008
Async XLA Ops:
  0.0 17.8 %collective-permute-start = (bf16[16,64,256]{2,1,0:T(8,128)(2,1)}, bf16[16,64,256]{2,1,0:T(8,128)(2,1)S(1)}, u32[]{:S(2)}, u32[]{:S(2)}) collective-permute-start(bf16[16,64,256]{2,1,0:T(8,128)(2,1)} %p_ref.1), channel_id=1, source_target_pairs={{0,1},{1,2},{2,3},{3,4},{4,5},{5,6},{6,7},{7,8},{8,9},{9,10},{10,1... | collective-permute-start | bytes 1572872 | tf_op jit(solution)/shard_map/ppermute | solution.py:16
  0.0 17.9 %collective-permute-start.1 = (bf16[16,64,256]{2,1,0:T(8,128)(2,1)}, bf16[16,64,256]{2,1,0:T(8,128)(2,1)S(1)}, u32[]{:S(2)}, u32[]{:S(2)}) collective-permute-start(bf16[16,64,256]{2,1,0:T(8,128)(2,1)} %p_ref.1), channel_id=1, source_target_pairs={{0,255},{1,0},{2,1},{3,2},{4,3},{5,4},{6,5},{7,6},{8,7},{9,8},{10,... | collective-permute-start | bytes 1572872 | tf_op jit(solution)/shard_map/ppermute | solution.py:16
  9.7 1.2 %copy-start = (bf16[16,64,448]{2,1,0:T(8,128)(2,1)S(1)}, bf16[16,64,448]{2,1,0:T(8,128)(2,1)}, u32[]{:S(2)}) copy-start(bf16[16,64,448]{2,1,0:T(8,128)(2,1)} %a_ref.1) | copy-start | bytes 2752516
  11.0 1.0 %copy-start.1 = (bf16[16,64,256]{2,1,0:T(8,128)(2,1)S(1)}, bf16[16,64,256]{2,1,0:T(8,128)(2,1)}, u32[]{:S(2)}) copy-start(bf16[16,64,256]{2,1,0:T(8,128)(2,1)} %p_ref.1) | copy-start | bytes 1572868
  20.3 10.4 %collective-permute-start.2 = (bf16[128,640]{1,0:T(8,128)(2,1)S(1)}, bf16[128,640]{1,0:T(8,128)(2,1)S(1)}, u32[]{:S(2)}, u32[]{:S(2)}) collective-permute-start(bf16[128,640]{1,0:T(8,128)(2,1)S(1)} %get-tuple-element.12), channel_id=1, source_target_pairs={{0,1},{1,2},{2,3},{3,4},{4,5},{5,6},{6,7},{7,8},{8,9},{9,10},{10,1... | collective-permute-start | bytes 491528 | tf_op jit(solution)/shard_map/ppermute | solution.py:16
  20.4 10.3 %collective-permute-start.3 = (bf16[128,640]{1,0:T(8,128)(2,1)S(1)}, bf16[128,640]{1,0:T(8,128)(2,1)S(1)}, u32[]{:S(2)}, u32[]{:S(2)}) collective-permute-start(bf16[128,640]{1,0:T(8,128)(2,1)S(1)} %get-tuple-element.14), channel_id=1, source_target_pairs={{0,255},{1,0},{2,1},{3,2},{4,3},{5,4},{6,5},{7,6},{8,7},{9,8},{10,... | collective-permute-start | bytes 491528 | tf_op jit(solution)/shard_map/ppermute | solution.py:16

commit v2 on v1

v2 whole, which is shorter than its diff:
```python
import jax
import jax.numpy as jnp
from jax import lax
from jax.experimental import pallas as pl
from jax.experimental.pallas import tpu as pltpu
from jax.sharding import PartitionSpec as P

AGS = 8
BS = 64
LANES = 128
VMEM_BYTES = 48 * 1024 * 1024
BOTH = ("grp", "row")


def shifted(value, axis, by):
    peers = lax.axis_size(axis)
    return lax.ppermute(value, axis, [(i, (i + by) % peers) for i in range(peers)])


def wrapped(value, total):
    value = jnp.where(value < 0, value + total, value)
    return jnp.where(value >= total, value - total, value)


def spread(blocks_ref, row, column_of, dense_ref):
    low = lax.broadcasted_iota(jnp.int32, (BS, LANES), 1) < BS
    for slot in range(blocks_ref.shape[2] // BS):
        block = blocks_ref[row, :, slot * BS : (slot + 1) * BS]
        twice = jnp.concatenate([block, block], axis=1)
        column = column_of(slot)
        place = dense_ref.at[column // 2, row * BS : (row + 1) * BS, :]
        place[...] = jnp.where(low == (column % 2 == 0), twice, place[...])


def joined(dense_ref, first, count):
    return jnp.concatenate([dense_ref[first + t] for t in range(count)], axis=1)


def columns_copy(columns_hbm, columns_ref, sem, group, rows):
    first = group * rows // LANES * LANES
    return pltpu.make_async_copy(
        columns_hbm.at[:, pl.ds(pl.multiple_of(first, LANES), LANES)], columns_ref, sem
    )


def left_kernel(
    a_cols_ref, columns_hbm, a_hbm, p_hbm, left_ref, own_ref,
    a_ref, p_ref, p_cols_ref, dense_a_ref, dense_p_ref, a_sem, p_sem, c_sem,
):
    rows = a_ref.shape[0]
    group = lax.axis_index(BOTH)
    groups = lax.axis_size(BOTH)
    fine_total = groups * rows
    aggregates = rows // AGS
    copy_c = columns_copy(columns_hbm, p_cols_ref, c_sem, group, rows)
    copy_p = pltpu.make_async_copy(p_hbm, p_ref, p_sem)
    copy_a = pltpu.make_async_copy(a_hbm, a_ref, a_sem)
    copy_c.start()
    copy_p.start()
    copy_a.start()
    dense_p_ref[...] = jnp.zeros_like(dense_p_ref)
    dense_a_ref[...] = jnp.zeros_like(dense_a_ref)
    copy_c.wait()
    copy_p.wait()
    lane = lax.rem(group * rows, LANES)
    for row in range(rows):
        spread(
            p_ref, row,
            lambda slot: wrapped(
                p_cols_ref[slot, lane + row] - (group - 1) * aggregates, groups * aggregates
            ),
            dense_p_ref,
        )
    tiles = dense_p_ref.shape[0]
    p_dense = joined(dense_p_ref, 0, tiles)
    p_turned = p_dense.T
    copy_a.wait()
    for row in range(rows):
        spread(
            a_ref, row,
            lambda slot: wrapped(a_cols_ref[slot, row] - (group - 1) * rows, fine_total),
            dense_a_ref,
        )
    parts = left_ref.shape[0]
    per_part = dense_a_ref.shape[0] // parts
    for part in range(parts):
        a_dense = joined(dense_a_ref, part * per_part, per_part)
        left_ref[part] = jnp.dot(
            p_turned, a_dense, preferred_element_type=jnp.float32
        ).astype(jnp.bfloat16)
    own_ref[...] = jnp.dot(left_ref[1], p_dense, preferred_element_type=jnp.float32)


def right_kernel(
    columns_hbm, before_ref, after_ref, left_ref, own_ref,
    to_before_ref, stay_ref, to_after_ref,
    before_cols_ref, after_cols_ref, dense_before_ref, dense_after_ref, b_sem, a_sem,
):
    rows = before_ref.shape[0]
    group = lax.axis_index(BOTH)
    groups = lax.axis_size(BOTH)
    aggregates = rows // AGS
    before = wrapped(group - 1, groups)
    after = wrapped(group + 1, groups)
    copy_b = columns_copy(columns_hbm, before_cols_ref, b_sem, before, rows)
    copy_a = columns_copy(columns_hbm, after_cols_ref, a_sem, after, rows)
    copy_b.start()
    copy_a.start()
    dense_before_ref[...] = jnp.zeros_like(dense_before_ref)
    dense_after_ref[...] = jnp.zeros_like(dense_after_ref)
    copy_b.wait()
    copy_a.wait()

    def fill(blocks_ref, cols_ref, source, dense_ref):
        lane = lax.rem(source * rows, LANES)
        for row in range(rows):
            spread(
                blocks_ref, row,
                lambda slot: wrapped(
                    cols_ref[slot, lane + row] - (source - 1) * aggregates, groups * aggregates
                ),
                dense_ref,
            )

    fill(before_ref, before_cols_ref, before, dense_before_ref)
    fill(after_ref, after_cols_ref, after, dense_after_ref)

    def term(part, dense_ref):
        dense = joined(dense_ref, 0, dense_ref.shape[0])
        return jnp.dot(left_ref[part], dense, preferred_element_type=jnp.float32)

    first = term(0, dense_before_ref)
    last = term(2, dense_after_ref)
    own = own_ref[...]
    step = LANES
    summed = jnp.concatenate(
        [
            first[:, :step],
            first[:, step : 2 * step] + own[:, :step],
            first[:, 2 * step :] + own[:, step : 2 * step] + last[:, :step],
            own[:, 2 * step :] + last[:, step : 2 * step],
            last[:, 2 * step :],
        ],
        axis=1,
    )
    side = stay_ref.shape[0]
    to_before_ref[...] = summed[:side].astype(to_before_ref.dtype)
    stay_ref[...] = summed[side : 2 * side]
    to_after_ref[...] = summed[2 * side :].astype(to_after_ref.dtype)


def assembled(pieces, offsets, rows, shape):
    def place_kernel(*refs):
        out_hbm, sems = refs[len(pieces)], refs[len(pieces) + 1]
        own = lax.axis_index("grp")
        size = lax.axis_size("grp")
        per_member = shape[0] // size
        copies = []
        for n in range(len(pieces)):
            first = lax.rem(own + offsets[n] + size, size) * per_member + rows[n]
            place = out_hbm.at[pl.ds(first, pieces[n].shape[0])]
            copies.append(pltpu.make_async_copy(refs[n], place, sems.at[n]))
        for copy in copies:
            copy.start()
        for copy in copies:
            copy.wait()

    vmem = pl.BlockSpec(memory_space=pltpu.VMEM)
    return pl.pallas_call(
        place_kernel,
        out_shape=jax.ShapeDtypeStruct(shape, jnp.bfloat16),
        in_specs=[vmem] * len(pieces),
        out_specs=pl.BlockSpec(memory_space=pltpu.HBM),
        scratch_shapes=[pltpu.SemaphoreType.DMA((len(pieces),))],
        compiler_params=pltpu.CompilerParams(vmem_limit_bytes=VMEM_BYTES),
        name="place_kernel",
    )(*pieces)


def per_device(matrix_blocks, matrix_columns, prolong_blocks, prolong_columns):
    rows = matrix_blocks.shape[0]
    aggregates = rows // AGS
    side = aggregates * BS
    before_blocks = shifted(prolong_blocks, BOTH, 1)
    after_blocks = shifted(prolong_blocks, BOTH, -1)
    columns_turned = pltpu.with_memory_space_constraint(prolong_columns.T, pltpu.HBM)
    matrix_kept = pltpu.with_memory_space_constraint(matrix_blocks, pltpu.HBM)
    prolong_kept = pltpu.with_memory_space_constraint(prolong_blocks, pltpu.HBM)
    matrix_turned = pltpu.with_memory_space_constraint(matrix_columns.T, pltpu.HBM)

    bf16 = jnp.bfloat16
    f32 = jnp.float32
    smem = pl.BlockSpec(memory_space=pltpu.SMEM)
    vmem = pl.BlockSpec(memory_space=pltpu.VMEM)
    hbm = pl.BlockSpec(memory_space=pltpu.HBM)
    sem = pltpu.SemaphoreType.DMA(())
    params = pltpu.CompilerParams(vmem_limit_bytes=VMEM_BYTES)
    columns_scratch = pltpu.SMEM((prolong_columns.shape[1], LANES), jnp.int32)
    dense = pltpu.VMEM((3 * side // LANES, rows * BS, LANES), bf16)
    left, own = pl.pallas_call(
        left_kernel,
        out_shape=(
            jax.ShapeDtypeStruct((3, 3 * side, rows * BS), bf16),
            jax.ShapeDtypeStruct((3 * side, 3 * side), f32),
        ),
        in_specs=[smem, hbm, hbm, hbm],
        out_specs=(vmem, vmem),
        scratch_shapes=[
            pltpu.VMEM(matrix_blocks.shape, bf16),
            pltpu.VMEM(prolong_blocks.shape, bf16),
            columns_scratch,
            pltpu.VMEM((3 * rows * BS // LANES, rows * BS, LANES), bf16),
            dense,
            sem, sem, sem,
        ],
        compiler_params=params,
        name="left_kernel",
    )(matrix_turned, columns_turned, matrix_kept, prolong_kept)

    to_before, stay, to_after = pl.pallas_call(
        right_kernel,
        out_shape=(
            jax.ShapeDtypeStruct((side, 5 * side), bf16),
            jax.ShapeDtypeStruct((side, 5 * side), f32),
            jax.ShapeDtypeStruct((side, 5 * side), bf16),
        ),
        in_specs=[hbm, vmem, vmem, vmem, vmem],
        out_specs=(vmem, vmem, vmem),
        scratch_shapes=[columns_scratch, columns_scratch, dense, dense, sem, sem],
        compiler_params=params,
        name="right_kernel",
    )(columns_turned, before_blocks, after_blocks, left, own)

    from_before = shifted(to_after, BOTH, 1)
    from_after = shifted(to_before, BOTH, -1)

    def widen(part, offset):
        return jnp.pad(part.astype(f32), ((0, 0), (offset * side, (2 - offset) * side)))

    total = widen(from_before, 0) + widen(stay, 1) + widen(from_after, 2)
    owned = total.astype(bf16).reshape(aggregates, BS, 7 * side)
    shape = (lax.axis_size("grp") * aggregates, BS, 7 * side)
    pieces = [owned] + [shifted(owned, "grp", by) for by in (1, -1, 2)]
    return assembled(pieces, (0, -1, 1, 2), (0, 0, 0, 0), shape)


def solution(mesh):
    placed = (
        P(("grp", "row"), None, None),
        P(("grp", "row"), None),
        P(("grp", "row"), None, None),
        P(),
    )
    return jax.shard_map(
        per_device, mesh=mesh, in_specs=placed, out_specs=P("row", None, None), check_vma=False
    )
```

time: 45.5 us -> 40.4 us (0.89)
  blocking collectives: 13.6 us -> 0 us
  waiting for transfers between devices: 3.11 us -> 12.1 us
  local copies, waits for them, and re-layouts: 3.19 us -> 0 us
  starting transfers between devices: 15.5 us -> 17.7 us
  Pallas kernels: 8.27 us -> 10.3 us
  other arithmetic: 1.59 us -> 0.05 us
    all_gather x1 -> x0, blocking collectives: 13.6 us -> none  [per_device(): return lax.all_gather(owned, 'grp', axis=0, tiled=True)]
    ppermute x4 -> x7, waiting for transfers between devices: 3.11 us -> 12.1 us  [shifted(): lax.ppermute(value, axis, [(i, (i + by) % peers) for i in range(peers)])]
    unnamed x5 -> x0, local copies, waits for them, and re-layouts: 3.19 us -> none
    ppermute x4 -> x7, starting transfers between devices: 15.5 us -> 17.7 us  [shifted(): lax.ppermute(value, axis, [(i, (i + by) % peers) for i in range(peers)])]
    select_n x2 -> x0, other arithmetic: 1.53 us -> none  [the longest x1 0.84 us: group_cols(): return jnp.mod(cols - (group - 1) * aggregates, coarse_total)]
    pallas_call x0 -> x1, Pallas kernels: none -> 0.95 us  [assembled(): pl.pallas_call(place_kernel, out_shape=jax.ShapeDtypeStruct(shape, jnp.bf...]
    pallas_call x1, Pallas kernels: 5.82 us -> 6.66 us  [per_device(): pl.pallas_call(left_kernel, out_shape=(jax.ShapeDtypeStruct((3, 3 * side,...]
  transfers between devices with their start and end apart: 4 -> 7, of which waited for: 1 -> 4; matrix products, arithmetic and copies ran while one was open for 3% -> 0% of each run, Pallas kernels for 13% -> 17%
where the time goes in v2:
time: 40.4 us; the launch traced here: 40.2 us
  starting transfers between devices  17.7 us (44%)
  waiting for transfers between devices  12.1 us (30%)
  Pallas kernels  10.3 us (25%)
    ppermute x7, starting transfers between devices, shifted(): lax.ppermute(value, axis, [(i, (i + by) % peers) for i in range(peers)])  17.7 us
    ppermute x7, waiting for transfers between devices, shifted(): lax.ppermute(value, axis, [(i, (i + by) % peers) for i in range(peers)])  12.1 us
    pallas_call x1, Pallas kernels, per_device(): pl.pallas_call(left_kernel, out_shape=(jax.ShapeDtypeStruct((3, 3 * side,...  6.66 us
    pallas_call x1, Pallas kernels, per_device(): pl.pallas_call(right_kernel, out_shape=(jax.ShapeDtypeStruct((side, 5 * s...  2.69 us
    pallas_call x1, Pallas kernels, assembled(): pl.pallas_call(place_kernel, out_shape=jax.ShapeDtypeStruct(shape, jnp.bf...  0.95 us
  transfers between devices with their start and end apart: 7, of which 4 were waited for; matrix products, arithmetic and copies ran while one was open for 0% of the time, Pallas kernels for 17%

profile of v2, /device:TPU:0, one launch (start us, length us, event | category | flops | bytes accessed | tf_op | source)
XLA Modules:
  0.0 40.2 jit_solution(3681746774857301077)
XLA Ops:
  0.0 0.0 collective-permute-start
  0.0 8.2 %collective-permute-start.1 = (bf16[16,64,256]{2,1,0:T(8,128)(2,1)}, bf16[16,64,256]{2,1,0:T(8,128)(2,1)S(1)}, u32[]{:S(2)}, u32[]{:S(2)}) collective-permute-start(bf16[16,64,256]{2,1,0:T(8,128)(2,1)} %p_hbm.1), channel_id=1, source_target_pairs={{0,255},{1,0},{2,1},{3,2},{4,3},{5,4},{6,5},{7,6},{8,7},{9,8},{10,... | collective-permute-start | bytes 1572872 | tf_op jit(solution)/shard_map/ppermute | solution.py:17
  8.2 6.7 %left_kernel.1 = (bf16[3,384,1024]{2,1,0:T(8,128)(2,1)S(1)}, f32[384,384]{1,0:T(8,128)S(1)}) custom-call(s32[7,16]{1,0:T(8,128)} %bitcast.9, s32[4,4096]{1,0:T(4,128)} %bitcast.7, bf16[16,64,448]{2,1,0:T(8,128)(2,1)} %a_hbm.1, bf16[16,64,256]{2,1,0:T(8,128)(2,1)} %p_hbm.1), custom_call_target="tpu_custom_call" | custom-call | tf_op jit(solution)/shard_map/left_kernel/pallas_call | solution.py:200
  14.9 0.4 %collective-permute-done.before_ref = bf16[16,64,256]{2,1,0:T(8,128)(2,1)S(1)} collective-permute-done((bf16[16,64,256]{2,1,0:T(8,128)(2,1)}, bf16[16,64,256]{2,1,0:T(8,128)(2,1)S(1)}, u32[]{:S(2)}, u32[]{:S(2)}) %collective-permute-start) | collective-permute-done | bytes 524320 | tf_op jit(solution)/shard_map/ppermute | solution.py:17
  15.3 0.0 collective-permute-done.1.after_ref
  15.3 2.7 %right_kernel.1 = (bf16[128,640]{1,0:T(8,128)(2,1)S(1)}, f32[128,640]{1,0:T(8,128)S(1)}, bf16[128,640]{1,0:T(8,128)(2,1)S(1)}) custom-call(s32[4,4096]{1,0:T(4,128)} %bitcast.8, bf16[16,64,256]{2,1,0:T(8,128)(2,1)S(1)} %collective-permute-done.before_ref, bf16[16,64,256]{2,1,0:T(8,128)(2,1)S(1)} %collective-permute-done.1.after_ref, ...), custom_call_target="tpu_custom_call" | custom-call | tf_op jit(solution)/shard_map/right_kernel/pallas_call | solution.py:220
  18.0 0.1 collective-permute-start.2
  18.1 7.2 %collective-permute-start.3 = (bf16[128,640]{1,0:T(8,128)(2,1)S(1)}, bf16[128,640]{1,0:T(8,128)(2,1)S(1)}, u32[]{:S(2)}, u32[]{:S(2)}) collective-permute-start(bf16[128,640]{1,0:T(8,128)(2,1)S(1)} %get-tuple-element.14), channel_id=1, source_target_pairs={{0,255},{1,0},{2,1},{3,2},{4,3},{5,4},{6,5},{7,6},{8,7},{9,8},{10,... | collective-permute-start | bytes 491528 | tf_op jit(solution)/shard_map/ppermute | solution.py:17
  25.3 3.8 %collective-permute-done.2 = bf16[128,640]{1,0:T(8,128)(2,1)S(1)} collective-permute-done((bf16[128,640]{1,0:T(8,128)(2,1)S(1)}, bf16[128,640]{1,0:T(8,128)(2,1)S(1)}, u32[]{:S(2)}, u32[]{:S(2)}) %collective-permute-start.2) | collective-permute-done | bytes 163872 | tf_op jit(solution)/shard_map/ppermute | solution.py:17
  29.1 0.0 collective-permute-done.3
  29.2 0.1 collective-permute-start.6
  29.3 0.1 collective-permute-start.5
  29.4 2.0 %collective-permute-start.4 = (bf16[2,64,896]{2,1,0:T(8,128)(2,1)S(1)}, bf16[2,64,896]{2,1,0:T(8,128)(2,1)S(1)}, u32[]{:S(2)}, u32[]{:S(2)}) collective-permute-start(bf16[2,64,896]{2,1,0:T(8,128)(2,1)S(1)} %bitcast.5), channel_id=1, source_target_pairs={{0,64},{64,128},{128,192},{192,0},{1,65},{65,129},{129,193},{193,1... | collective-permute-start | bytes 688136 | tf_op jit(solution)/shard_map/ppermute | solution.py:17
  31.4 5.5 %collective-permute-done.6.refs_3_ = bf16[2,64,896]{2,1,0:T(8,128)(2,1)S(1)} collective-permute-done((bf16[2,64,896]{2,1,0:T(8,128)(2,1)S(1)}, bf16[2,64,896]{2,1,0:T(8,128)(2,1)S(1)}, u32[]{:S(2)}, u32[]{:S(2)}) %collective-permute-start.6) | collective-permute-done | bytes 229408 | tf_op jit(solution)/shard_map/ppermute | solution.py:17
  36.9 0.0 collective-permute-done.5.refs_2_
  36.9 2.4 %collective-permute-done.4.refs_1_ = bf16[2,64,896]{2,1,0:T(8,128)(2,1)S(1)} collective-permute-done((bf16[2,64,896]{2,1,0:T(8,128)(2,1)S(1)}, bf16[2,64,896]{2,1,0:T(8,128)(2,1)S(1)}, u32[]{:S(2)}, u32[]{:S(2)}) %collective-permute-start.4) | collective-permute-done | bytes 229408 | tf_op jit(solution)/shard_map/ppermute | solution.py:17
  39.3 0.9 %place_kernel.1 = bf16[8,64,896]{2,1,0:T(8,128)(2,1)} custom-call(bf16[2,64,896]{2,1,0:T(8,128)(2,1)S(1)} %bitcast.6, bf16[2,64,896]{2,1,0:T(8,128)(2,1)S(1)} %collective-permute-done.4.refs_1_, bf16[2,64,896]{2,1,0:T(8,128)(2,1)S(1)} %collective-permute-done.5.refs_2_, bf16[2,64,896]{2,1,0:T(8,128)(2,1)S(1)} %collective-permute-done.6.refs_3_), custom_call_target="tpu_custom_call" | custom-call | tf_op jit(solution)/shard_map/place_kernel/pallas_call | solution.py:169
  (1 shorter events, 0.0 us)
Async XLA Ops:
  0.0 15.3 %collective-permute-start = (bf16[16,64,256]{2,1,0:T(8,128)(2,1)}, bf16[16,64,256]{2,1,0:T(8,128)(2,1)S(1)}, u32[]{:S(2)}, u32[]{:S(2)}) collective-permute-start(bf16[16,64,256]{2,1,0:T(8,128)(2,1)} %p_hbm.1), channel_id=1, source_target_pairs={{0,1},{1,2},{2,3},{3,4},{4,5},{5,6},{6,7},{7,8},{8,9},{9,10},{10,1... | collective-permute-start | bytes 1572872 | tf_op jit(solution)/shard_map/ppermute | solution.py:17
  0.0 15.3 %collective-permute-start.1 = (bf16[16,64,256]{2,1,0:T(8,128)(2,1)}, bf16[16,64,256]{2,1,0:T(8,128)(2,1)S(1)}, u32[]{:S(2)}, u32[]{:S(2)}) collective-permute-start(bf16[16,64,256]{2,1,0:T(8,128)(2,1)} %p_hbm.1), channel_id=1, source_target_pairs={{0,255},{1,0},{2,1},{3,2},{4,3},{5,4},{6,5},{7,6},{8,7},{9,8},{10,... | collective-permute-start | bytes 1572872 | tf_op jit(solution)/shard_map/ppermute | solution.py:17
  18.0 11.1 %collective-permute-start.2 = (bf16[128,640]{1,0:T(8,128)(2,1)S(1)}, bf16[128,640]{1,0:T(8,128)(2,1)S(1)}, u32[]{:S(2)}, u32[]{:S(2)}) collective-permute-start(bf16[128,640]{1,0:T(8,128)(2,1)S(1)} %get-tuple-element.12), channel_id=1, source_target_pairs={{0,1},{1,2},{2,3},{3,4},{4,5},{5,6},{6,7},{7,8},{8,9},{9,10},{10,1... | collective-permute-start | bytes 491528 | tf_op jit(solution)/shard_map/ppermute | solution.py:17
  18.1 11.1 %collective-permute-start.3 = (bf16[128,640]{1,0:T(8,128)(2,1)S(1)}, bf16[128,640]{1,0:T(8,128)(2,1)S(1)}, u32[]{:S(2)}, u32[]{:S(2)}) collective-permute-start(bf16[128,640]{1,0:T(8,128)(2,1)S(1)} %get-tuple-element.14), channel_id=1, source_target_pairs={{0,255},{1,0},{2,1},{3,2},{4,3},{5,4},{6,5},{7,6},{8,7},{9,8},{10,... | collective-permute-start | bytes 491528 | tf_op jit(solution)/shard_map/ppermute | solution.py:17
  29.2 7.7 %collective-permute-start.6 = (bf16[2,64,896]{2,1,0:T(8,128)(2,1)S(1)}, bf16[2,64,896]{2,1,0:T(8,128)(2,1)S(1)}, u32[]{:S(2)}, u32[]{:S(2)}) collective-permute-start(bf16[2,64,896]{2,1,0:T(8,128)(2,1)S(1)} %bitcast.3), channel_id=1, source_target_pairs={{0,128},{64,192},{128,0},{192,64},{1,129},{65,193},{129,1},{193,65... | collective-permute-start | bytes 688136 | tf_op jit(solution)/shard_map/ppermute | solution.py:17
  29.3 7.6 %collective-permute-start.5 = (bf16[2,64,896]{2,1,0:T(8,128)(2,1)S(1)}, bf16[2,64,896]{2,1,0:T(8,128)(2,1)S(1)}, u32[]{:S(2)}, u32[]{:S(2)}) collective-permute-start(bf16[2,64,896]{2,1,0:T(8,128)(2,1)S(1)} %bitcast.4), channel_id=1, source_target_pairs={{0,192},{64,0},{128,64},{192,128},{1,193},{65,1},{129,65},{193,129... | collective-permute-start | bytes 688136 | tf_op jit(solution)/shard_map/ppermute | solution.py:17
  29.4 9.9 %collective-permute-start.4 = (bf16[2,64,896]{2,1,0:T(8,128)(2,1)S(1)}, bf16[2,64,896]{2,1,0:T(8,128)(2,1)S(1)}, u32[]{:S(2)}, u32[]{:S(2)}) collective-permute-start(bf16[2,64,896]{2,1,0:T(8,128)(2,1)S(1)} %bitcast.5), channel_id=1, source_target_pairs={{0,64},{64,128},{128,192},{192,0},{1,65},{65,129},{129,193},{193,1... | collective-permute-start | bytes 688136 | tf_op jit(solution)/shard_map/ppermute | solution.py:17

commit v3 on v2

--- a/solution.py
+++ b/solution.py
@@ -43,9 +43,52 @@
     )
 
 
+def mark(columns_ref, group, groups, rows, mask_ref, first):
+    aggregates = rows // AGS
+    slots = columns_ref.shape[0]
+    block = lax.broadcasted_iota(jnp.int32, mask_ref.shape[1:], 1) // BS
+    lane = lax.rem(group * rows, LANES)
+    for row in range(rows):
+        for slot in range(slots):
+            column = wrapped(
+                columns_ref[slot, lane + row] - (group - 1) * aggregates, groups * aggregates
+            )
+            mask_ref[first + row * slots + slot] = jnp.where(block == column, 1.0, 0.0).astype(
+                mask_ref.dtype
+            )
+
+
+def dense_rows(blocks_ref, mask_ref, first):
+    rows, _, width = blocks_ref.shape
+    slots = width // BS
+    packed = mask_ref.shape[1]
+    low = lax.broadcasted_iota(jnp.int32, (BS, LANES), 1) < BS
+    parts = []
+    for row in range(rows):
+        twice = []
+        for pair in range(slots // 2):
+            both = blocks_ref[row, :, pair * LANES : (pair + 1) * LANES]
+            swapped = jnp.concatenate([both[:, BS:], both[:, :BS]], axis=1)
+            twice.append(jnp.where(low, both, swapped))
+            twice.append(jnp.where(low, swapped, both))
+        tiles = []
+        for tile in range(mask_ref.shape[2] // LANES):
+            total = None
+            for slot in range(slots):
+                mask = mask_ref[
+                    first + row * slots + slot, :, tile * LANES : (tile + 1) * LANES
+                ]
+                term = twice[slot].reshape(BS // packed, packed, LANES) * mask[None]
+                total = term if total is None else total + term
+            tiles.append(total.reshape(BS, LANES))
+        parts.append(jnp.concatenate(tiles, axis=1))
+    return jnp.concatenate(parts, axis=0)
+
+
 def left_kernel(
-    a_cols_ref, columns_hbm, a_hbm, p_hbm, left_ref, own_ref,
-    a_ref, p_ref, p_cols_ref, dense_a_ref, dense_p_ref, a_sem, p_sem, c_sem,
+    a_cols_ref, columns_hbm, a_hbm, p_hbm, left_ref, own_ref, mask_ref,
+    a_ref, p_ref, p_cols_ref, before_cols_ref, after_cols_ref, dense_a_ref, dense_p_ref,
+    a_sem, p_sem, c_sem, before_sem, after_sem,
 ):
     rows = a_ref.shape[0]
     group = lax.axis_index(BOTH)
@@ -55,9 +98,15 @@
     copy_c = columns_copy(columns_hbm, p_cols_ref, c_sem, group, rows)
     copy_p = pltpu.make_async_copy(p_hbm, p_ref, p_sem)
     copy_a = pltpu.make_async_copy(a_hbm, a_ref, a_sem)
+    before = wrapped(group - 1, groups)
+    after = wrapped(group + 1, groups)
+    copy_before = columns_copy(columns_hbm, before_cols_ref, before_sem, before, rows)
+    copy_after = columns_copy(columns_hbm, after_cols_ref, after_sem, after, rows)
     copy_c.start()
     copy_p.start()
     copy_a.start()
+    copy_before.start()
+    copy_after.start()
     dense_p_ref[...] = jnp.zeros_like(dense_p_ref)
     dense_a_ref[...] = jnp.zeros_like(dense_a_ref)
     copy_c.wait()
@@ -89,48 +138,21 @@
             p_turned, a_dense, preferred_element_type=jnp.float32
         ).astype(jnp.bfloat16)
     own_ref[...] = jnp.dot(left_ref[1], p_dense, preferred_element_type=jnp.float32)
+    copy_before.wait()
+    copy_after.wait()
+    mark(before_cols_ref, before, groups, rows, mask_ref, 0)
+    mark(after_cols_ref, after, groups, rows, mask_ref, mask_ref.shape[0] // 2)
 
 
 def right_kernel(
-    columns_hbm, before_ref, after_ref, left_ref, own_ref,
-    to_before_ref, stay_ref, to_after_ref,
-    before_cols_ref, after_cols_ref, dense_before_ref, dense_after_ref, b_sem, a_sem,
+    before_ref, after_ref, mask_ref, left_ref, own_ref, to_before_ref, stay_ref, to_after_ref
 ):
-    rows = before_ref.shape[0]
-    group = lax.axis_index(BOTH)
-    groups = lax.axis_size(BOTH)
-    aggregates = rows // AGS
-    before = wrapped(group - 1, groups)
-    after = wrapped(group + 1, groups)
-    copy_b = columns_copy(columns_hbm, before_cols_ref, b_sem, before, rows)
-    copy_a = columns_copy(columns_hbm, after_cols_ref, a_sem, after, rows)
-    copy_b.start()
-    copy_a.start()
-    dense_before_ref[...] = jnp.zeros_like(dense_before_ref)
-    dense_after_ref[...] = jnp.zeros_like(dense_after_ref)
-    copy_b.wait()
-    copy_a.wait()
-
-    def fill(blocks_ref, cols_ref, source, dense_ref):
-        lane = lax.rem(source * rows, LANES)
-        for row in range(rows):
-            spread(
-                blocks_ref, row,
-                lambda slot: wrapped(
-                    cols_ref[slot, lane + row] - (source - 1) * aggregates, groups * aggregates
-                ),
-                dense_ref,
-            )
-
-    fill(before_ref, before_cols_ref, before, dense_before_ref)
-    fill(after_ref, after_cols_ref, after, dense_after_ref)
-
-    def term(part, dense_ref):
-        dense = joined(dense_ref, 0, dense_ref.shape[0])
+    def term(part, blocks_ref, first_mask):
+        dense = dense_rows(blocks_ref, mask_ref, first_mask)
         return jnp.dot(left_ref[part], dense, preferred_element_type=jnp.float32)
 
-    first = term(0, dense_before_ref)
-    last = term(2, dense_after_ref)
+    first = term(0, before_ref, 0)
+    last = term(2, after_ref, mask_ref.shape[0] // 2)
     own = own_ref[...]
     step = LANES
     summed = jnp.concatenate(
@@ -149,9 +171,11 @@
     to_after_ref[...] = summed[2 * side :].astype(to_after_ref.dtype)
 
 
-def assembled(pieces, offsets, rows, shape):
+def placed(out, pieces, offsets, rows, shape):
+    given = () if out is None else (out,)
+
     def place_kernel(*refs):
-        out_hbm, sems = refs[len(pieces)], refs[len(pieces) + 1]
+        out_hbm, sems = refs[-2], refs[-1]
         own = lax.axis_index("grp")
         size = lax.axis_size("grp")
         per_member = shape[0] // size
@@ -159,22 +183,24 @@
         for n in range(len(pieces)):
             first = lax.rem(own + offsets[n] + size, size) * per_member + rows[n]
             place = out_hbm.at[pl.ds(first, pieces[n].shape[0])]
-            copies.append(pltpu.make_async_copy(refs[n], place, sems.at[n]))
+            copies.append(pltpu.make_async_copy(refs[len(given) + n], place, sems.at[n]))
         for copy in copies:
             copy.start()
         for copy in copies:
             copy.wait()
 
     vmem = pl.BlockSpec(memory_space=pltpu.VMEM)
+    hbm = pl.BlockSpec(memory_space=pltpu.HBM)
     return pl.pallas_call(
         place_kernel,
         out_shape=jax.ShapeDtypeStruct(shape, jnp.bfloat16),
-        in_specs=[vmem] * len(pieces),
-        out_specs=pl.BlockSpec(memory_space=pltpu.HBM),
+        in_specs=[hbm] * len(given) + [vmem] * len(pieces),
+        out_specs=hbm,
         scratch_shapes=[pltpu.SemaphoreType.DMA((len(pieces),))],
+        input_output_aliases={0: 0} if given else {},
         compiler_params=pltpu.CompilerParams(vmem_limit_bytes=VMEM_BYTES),
         name="place_kernel",
-    )(*pieces)
+    )(*given, *pieces)
 
 
 def per_device(matrix_blocks, matrix_columns, prolong_blocks, prolong_columns):
@@ -197,21 +223,24 @@
     params = pltpu.CompilerParams(vmem_limit_bytes=VMEM_BYTES)
     columns_scratch = pltpu.SMEM((prolong_columns.shape[1], LANES), jnp.int32)
     dense = pltpu.VMEM((3 * side // LANES, rows * BS, LANES), bf16)
-    left, own = pl.pallas_call(
+    slots = prolong_columns.shape[1]
+    packed = 16
+    left, own, masks = pl.pallas_call(
         left_kernel,
         out_shape=(
             jax.ShapeDtypeStruct((3, 3 * side, rows * BS), bf16),
             jax.ShapeDtypeStruct((3 * side, 3 * side), f32),
+            jax.ShapeDtypeStruct((2 * rows * slots, packed, 3 * side), bf16),
         ),
         in_specs=[smem, hbm, hbm, hbm],
-        out_specs=(vmem, vmem),
+        out_specs=(vmem, vmem, vmem),
         scratch_shapes=[
             pltpu.VMEM(matrix_blocks.shape, bf16),
             pltpu.VMEM(prolong_blocks.shape, bf16),
-            columns_scratch,
+            columns_scratch, columns_scratch, columns_scratch,
             pltpu.VMEM((3 * rows * BS // LANES, rows * BS, LANES), bf16),
             dense,
-            sem, sem, sem,
+            sem, sem, sem, sem, sem,
         ],
         compiler_params=params,
         name="left_kernel",
@@ -224,12 +253,11 @@
             jax.ShapeDtypeStruct((side, 5 * side), f32),
             jax.ShapeDtypeStruct((side, 5 * side), bf16),
         ),
-        in_specs=[hbm, vmem, vmem, vmem, vmem],
+        in_specs=[vmem, vmem, vmem, vmem, vmem],
         out_specs=(vmem, vmem, vmem),
-        scratch_shapes=[columns_scratch, columns_scratch, dense, dense, sem, sem],
         compiler_params=params,
         name="right_kernel",
-    )(columns_turned, before_blocks, after_blocks, left, own)
+    )(before_blocks, after_blocks, masks, left, own)
 
     from_before = shifted(to_after, BOTH, 1)
     from_after = shifted(to_before, BOTH, -1)
@@ -240,8 +268,9 @@
     total = widen(from_before, 0) + widen(stay, 1) + widen(from_after, 2)
     owned = total.astype(bf16).reshape(aggregates, BS, 7 * side)
     shape = (lax.axis_size("grp") * aggregates, BS, 7 * side)
-    pieces = [owned] + [shifted(owned, "grp", by) for by in (1, -1, 2)]
-    return assembled(pieces, (0, -1, 1, 2), (0, 0, 0, 0), shape)
+    below, above, far = [shifted(owned, "grp", by) for by in (1, -1, 2)]
+    out = placed(None, [owned, above, far], (0, 1, 2), (0, 0, 0), shape)
+    return placed(out, [below], (-1,), (0,), shape)
 
 
 def solution(mesh):

time: 40.4 us -> 38.9 us (0.963)
  waiting for transfers between devices: 12.1 us -> 10.8 us
    ppermute x7, waiting for transfers between devices: 12.1 us -> 10.8 us  [shifted(): lax.ppermute(value, axis, [(i, (i + by) % peers) for i in range(peers)])]
    pallas_call x1, Pallas kernels: 2.69 us -> 1.55 us  [per_device(): pl.pallas_call(right_kernel, out_shape=(jax.ShapeDtypeStruct((side, 5 * s...]
    pallas_call x1 -> x2, Pallas kernels: 0.95 us -> 1.56 us  [placed(): pl.pallas_call(place_kernel, out_shape=jax.ShapeDtypeStruct(shape, jnp.bf...]
    pallas_call x1, Pallas kernels: 6.66 us -> 7.06 us  [per_device(): pl.pallas_call(left_kernel, out_shape=(jax.ShapeDtypeStruct((3, 3 * side,...]
  transfers between devices with their start and end apart: 7 -> 7, of which waited for: 4 -> 3; matrix products, arithmetic and copies ran while one was open for 0% -> 0% of each run, Pallas kernels for 17% -> 20%
where the time goes in v3:
time: 38.9 us; the launch traced here: 38.8 us
  starting transfers between devices  17.7 us (46%)
  waiting for transfers between devices  10.8 us (28%)
  Pallas kernels  10.2 us (26%)
    ppermute x7, starting transfers between devices, shifted(): lax.ppermute(value, axis, [(i, (i + by) % peers) for i in range(peers)])  17.7 us
    ppermute x7, waiting for transfers between devices, shifted(): lax.ppermute(value, axis, [(i, (i + by) % peers) for i in range(peers)])  10.8 us
    pallas_call x1, Pallas kernels, per_device(): pl.pallas_call(left_kernel, out_shape=(jax.ShapeDtypeStruct((3, 3 * side,...  7.06 us
    pallas_call x2, Pallas kernels, placed(): pl.pallas_call(place_kernel, out_shape=jax.ShapeDtypeStruct(shape, jnp.bf...  1.56 us
    pallas_call x1, Pallas kernels, per_device(): pl.pallas_call(right_kernel, out_shape=(jax.ShapeDtypeStruct((side, 5 * s...  1.55 us
  transfers between devices with their start and end apart: 7, of which 3 were waited for; matrix products, arithmetic and copies ran while one was open for 0% of the time, Pallas kernels for 20%

profile of v3, /device:TPU:0, one launch (start us, length us, event | category | flops | bytes accessed | tf_op | source)
XLA Modules:
  0.0 38.8 jit_solution(8601173908897594410)
XLA Ops:
  0.0 0.0 collective-permute-start
  0.0 8.2 %collective-permute-start.1 = (bf16[16,64,256]{2,1,0:T(8,128)(2,1)}, bf16[16,64,256]{2,1,0:T(8,128)(2,1)S(1)}, u32[]{:S(2)}, u32[]{:S(2)}) collective-permute-start(bf16[16,64,256]{2,1,0:T(8,128)(2,1)} %p_hbm.1), channel_id=1, source_target_pairs={{0,255},{1,0},{2,1},{3,2},{4,3},{5,4},{6,5},{7,6},{8,7},{9,8},{10,... | collective-permute-start | bytes 1572872 | tf_op jit(solution)/shard_map/ppermute | solution.py:17
  8.2 7.1 %left_kernel.1 = (bf16[3,384,1024]{2,1,0:T(8,128)(2,1)S(1)}, f32[384,384]{1,0:T(8,128)S(1)}, bf16[128,16,384]{2,1,0:T(8,128)(2,1)S(1)}) custom-call(s32[7,16]{1,0:T(8,128)} %bitcast.8, s32[4,4096]{1,0:T(4,128)} %bitcast.7, bf16[16,64,448]{2,1,0:T(8,128)(2,1)} %a_hbm.1, bf16[16,64,256]{2,1,0:T(8,128)(2,1)} %p_hbm.1), custom_call_target="tpu_custom_call" | custom-call | tf_op jit(solution)/shard_map/left_kernel/pallas_call | solution.py:228
  15.3 0.0 collective-permute-done.before_ref
  15.3 0.0 collective-permute-done.1.after_ref
  15.3 1.6 %right_kernel.1 = (bf16[128,640]{1,0:T(8,128)(2,1)S(1)}, f32[128,640]{1,0:T(8,128)S(1)}, bf16[128,640]{1,0:T(8,128)(2,1)S(1)}) custom-call(bf16[16,64,256]{2,1,0:T(8,128)(2,1)S(1)} %collective-permute-done.before_ref, bf16[16,64,256]{2,1,0:T(8,128)(2,1)S(1)} %collective-permute-done.1.after_ref, bf16[128,16,384]{2,1,0:T(8,128)(2,1)S(1)} %get-tuple-element.11.mask_ref, ...), custom_call_target="tpu_custom_call" | custom-call | tf_op jit(solution)/shard_map/right_kernel/pallas_call | solution.py:249
  16.9 0.1 collective-permute-start.2
  16.9 7.2 %collective-permute-start.3 = (bf16[128,640]{1,0:T(8,128)(2,1)S(1)}, bf16[128,640]{1,0:T(8,128)(2,1)S(1)}, u32[]{:S(2)}, u32[]{:S(2)}) collective-permute-start(bf16[128,640]{1,0:T(8,128)(2,1)S(1)} %get-tuple-element.16), channel_id=1, source_target_pairs={{0,255},{1,0},{2,1},{3,2},{4,3},{5,4},{6,5},{7,6},{8,7},{9,8},{10,... | collective-permute-start | bytes 491528 | tf_op jit(solution)/shard_map/ppermute | solution.py:17
  24.2 3.8 %collective-permute-done.2 = bf16[128,640]{1,0:T(8,128)(2,1)S(1)} collective-permute-done((bf16[128,640]{1,0:T(8,128)(2,1)S(1)}, bf16[128,640]{1,0:T(8,128)(2,1)S(1)}, u32[]{:S(2)}, u32[]{:S(2)}) %collective-permute-start.2) | collective-permute-done | bytes 163872 | tf_op jit(solution)/shard_map/ppermute | solution.py:17
  28.0 0.0 collective-permute-done.3
  28.1 0.1 collective-permute-start.5
  28.2 0.1 collective-permute-start.4
  28.2 2.0 %collective-permute-start.6 = (bf16[2,64,896]{2,1,0:T(8,128)(2,1)S(1)}, bf16[2,64,896]{2,1,0:T(8,128)(2,1)S(1)}, u32[]{:S(2)}, u32[]{:S(2)}) collective-permute-start(bf16[2,64,896]{2,1,0:T(8,128)(2,1)S(1)} %bitcast.5), channel_id=1, source_target_pairs={{0,64},{64,128},{128,192},{192,0},{1,65},{65,129},{129,193},{193,1... | collective-permute-start | bytes 688136 | tf_op jit(solution)/shard_map/ppermute | solution.py:17
  30.3 5.5 %collective-permute-done.5.refs_2_ = bf16[2,64,896]{2,1,0:T(8,128)(2,1)S(1)} collective-permute-done((bf16[2,64,896]{2,1,0:T(8,128)(2,1)S(1)}, bf16[2,64,896]{2,1,0:T(8,128)(2,1)S(1)}, u32[]{:S(2)}, u32[]{:S(2)}) %collective-permute-start.5) | collective-permute-done | bytes 229408 | tf_op jit(solution)/shard_map/ppermute | solution.py:17
  35.8 0.0 collective-permute-done.4.refs_1_
  35.8 0.9 %place_kernel.2.refs_0_ = bf16[8,64,896]{2,1,0:T(8,128)(2,1)} custom-call(bf16[2,64,896]{2,1,0:T(8,128)(2,1)S(1)} %bitcast.6, bf16[2,64,896]{2,1,0:T(8,128)(2,1)S(1)} %collective-permute-done.4.refs_1_, bf16[2,64,896]{2,1,0:T(8,128)(2,1)S(1)} %collective-permute-done.5.refs_2_), custom_call_target="tpu_custom_call" | custom-call | tf_op jit(solution)/shard_map/place_kernel/pallas_call | solution.py:194
  36.6 1.5 %collective-permute-done.6.refs_1_ = bf16[2,64,896]{2,1,0:T(8,128)(2,1)S(1)} collective-permute-done((bf16[2,64,896]{2,1,0:T(8,128)(2,1)S(1)}, bf16[2,64,896]{2,1,0:T(8,128)(2,1)S(1)}, u32[]{:S(2)}, u32[]{:S(2)}) %collective-permute-start.6) | collective-permute-done | bytes 229408 | tf_op jit(solution)/shard_map/ppermute | solution.py:17
  38.1 0.7 %place_kernel.3 = bf16[8,64,896]{2,1,0:T(8,128)(2,1)} custom-call(bf16[8,64,896]{2,1,0:T(8,128)(2,1)} %place_kernel.2.refs_0_, bf16[2,64,896]{2,1,0:T(8,128)(2,1)S(1)} %collective-permute-done.6.refs_1_), custom_call_target="tpu_custom_call", output_to_operand_aliasing={{}: (0, {})} | custom-call | tf_op jit(solution)/shard_map/place_kernel/pallas_call | solution.py:194
  (1 shorter events, 0.0 us)
Async XLA Ops:
  0.0 15.3 %collective-permute-start = (bf16[16,64,256]{2,1,0:T(8,128)(2,1)}, bf16[16,64,256]{2,1,0:T(8,128)(2,1)S(1)}, u32[]{:S(2)}, u32[]{:S(2)}) collective-permute-start(bf16[16,64,256]{2,1,0:T(8,128)(2,1)} %p_hbm.1), channel_id=1, source_target_pairs={{0,1},{1,2},{2,3},{3,4},{4,5},{5,6},{6,7},{7,8},{8,9},{9,10},{10,1... | collective-permute-start | bytes 1572872 | tf_op jit(solution)/shard_map/ppermute | solution.py:17
  0.0 15.3 %collective-permute-start.1 = (bf16[16,64,256]{2,1,0:T(8,128)(2,1)}, bf16[16,64,256]{2,1,0:T(8,128)(2,1)S(1)}, u32[]{:S(2)}, u32[]{:S(2)}) collective-permute-start(bf16[16,64,256]{2,1,0:T(8,128)(2,1)} %p_hbm.1), channel_id=1, source_target_pairs={{0,255},{1,0},{2,1},{3,2},{4,3},{5,4},{6,5},{7,6},{8,7},{9,8},{10,... | collective-permute-start | bytes 1572872 | tf_op jit(solution)/shard_map/ppermute | solution.py:17
  16.9 11.1 %collective-permute-start.2 = (bf16[128,640]{1,0:T(8,128)(2,1)S(1)}, bf16[128,640]{1,0:T(8,128)(2,1)S(1)}, u32[]{:S(2)}, u32[]{:S(2)}) collective-permute-start(bf16[128,640]{1,0:T(8,128)(2,1)S(1)} %get-tuple-element.14), channel_id=1, source_target_pairs={{0,1},{1,2},{2,3},{3,4},{4,5},{5,6},{6,7},{7,8},{8,9},{9,10},{10,1... | collective-permute-start | bytes 491528 | tf_op jit(solution)/shard_map/ppermute | solution.py:17
  16.9 11.1 %collective-permute-start.3 = (bf16[128,640]{1,0:T(8,128)(2,1)S(1)}, bf16[128,640]{1,0:T(8,128)(2,1)S(1)}, u32[]{:S(2)}, u32[]{:S(2)}) collective-permute-start(bf16[128,640]{1,0:T(8,128)(2,1)S(1)} %get-tuple-element.16), channel_id=1, source_target_pairs={{0,255},{1,0},{2,1},{3,2},{4,3},{5,4},{6,5},{7,6},{8,7},{9,8},{10,... | collective-permute-start | bytes 491528 | tf_op jit(solution)/shard_map/ppermute | solution.py:17
  28.1 7.7 %collective-permute-start.5 = (bf16[2,64,896]{2,1,0:T(8,128)(2,1)S(1)}, bf16[2,64,896]{2,1,0:T(8,128)(2,1)S(1)}, u32[]{:S(2)}, u32[]{:S(2)}) collective-permute-start(bf16[2,64,896]{2,1,0:T(8,128)(2,1)S(1)} %bitcast.3), channel_id=1, source_target_pairs={{0,128},{64,192},{128,0},{192,64},{1,129},{65,193},{129,1},{193,65... | collective-permute-start | bytes 688136 | tf_op jit(solution)/shard_map/ppermute | solution.py:17
  28.2 7.6 %collective-permute-start.4 = (bf16[2,64,896]{2,1,0:T(8,128)(2,1)S(1)}, bf16[2,64,896]{2,1,0:T(8,128)(2,1)S(1)}, u32[]{:S(2)}, u32[]{:S(2)}) collective-permute-start(bf16[2,64,896]{2,1,0:T(8,128)(2,1)S(1)} %bitcast.4), channel_id=1, source_target_pairs={{0,192},{64,0},{128,64},{192,128},{1,193},{65,1},{129,65},{193,129... | collective-permute-start | bytes 688136 | tf_op jit(solution)/shard_map/ppermute | solution.py:17
  28.2 9.9 %collective-permute-start.6 = (bf16[2,64,896]{2,1,0:T(8,128)(2,1)S(1)}, bf16[2,64,896]{2,1,0:T(8,128)(2,1)S(1)}, u32[]{:S(2)}, u32[]{:S(2)}) collective-permute-start(bf16[2,64,896]{2,1,0:T(8,128)(2,1)S(1)} %bitcast.5), channel_id=1, source_target_pairs={{0,64},{64,128},{128,192},{192,0},{1,65},{65,129},{129,193},{193,1... | collective-permute-start | bytes 688136 | tf_op jit(solution)/shard_map/ppermute | solution.py:17

commit v4 on v3

--- a/solution.py
+++ b/solution.py
@@ -48,29 +48,30 @@
     slots = columns_ref.shape[0]
     block = lax.broadcasted_iota(jnp.int32, mask_ref.shape[1:], 1) // BS
     lane = lax.rem(group * rows, LANES)
-    for row in range(rows):
-        for slot in range(slots):
-            column = wrapped(
-                columns_ref[slot, lane + row] - (group - 1) * aggregates, groups * aggregates
-            )
-            mask_ref[first + row * slots + slot] = jnp.where(block == column, 1.0, 0.0).astype(
-                mask_ref.dtype
-            )
+    low = lax.rem(lax.broadcasted_iota(jnp.int32, mask_ref.shape[1:], 1), LANES) < BS
+    for row in range(rows):
+        for slot in range(0, slots, 2):
+            even, odd = [
+                wrapped(columns_ref[n, lane + row] - (group - 1) * aggregates, groups * aggregates)
+                for n in (slot, slot + 1)
+            ]
+            for n, column in enumerate((jnp.where(low, even, odd), jnp.where(low, odd, even))):
+                mask_ref[first + row * slots + slot + n] = jnp.where(
+                    block == column, 1.0, 0.0
+                ).astype(mask_ref.dtype)
 
 
 def dense_rows(blocks_ref, mask_ref, first):
     rows, _, width = blocks_ref.shape
     slots = width // BS
     packed = mask_ref.shape[1]
-    low = lax.broadcasted_iota(jnp.int32, (BS, LANES), 1) < BS
     parts = []
     for row in range(rows):
         twice = []
         for pair in range(slots // 2):
             both = blocks_ref[row, :, pair * LANES : (pair + 1) * LANES]
             swapped = jnp.concatenate([both[:, BS:], both[:, :BS]], axis=1)
-            twice.append(jnp.where(low, both, swapped))
-            twice.append(jnp.where(low, swapped, both))
+            twice += [both, swapped]
         tiles = []
         for tile in range(mask_ref.shape[2] // LANES):
             total = None

time: 38.9 us -> 38.7 us (level)
  transfers between devices with their start and end apart: 7 -> 7, of which waited for: 3 -> 3; matrix products, arithmetic and copies ran while one was open for 0% -> 0% of each run, Pallas kernels for 20% -> 21%
where the time goes in v4:
time: 38.7 us; the launch traced here: 38.6 us
  starting transfers between devices  17.7 us (46%)
  waiting for transfers between devices  10.8 us (28%)
  Pallas kernels  9.98 us (26%)
    ppermute x7, starting transfers between devices, shifted(): lax.ppermute(value, axis, [(i, (i + by) % peers) for i in range(peers)])  17.7 us
    ppermute x7, waiting for transfers between devices, shifted(): lax.ppermute(value, axis, [(i, (i + by) % peers) for i in range(peers)])  10.8 us
    pallas_call x1, Pallas kernels, per_device(): pl.pallas_call(left_kernel, out_shape=(jax.ShapeDtypeStruct((3, 3 * side,...  7.05 us
    pallas_call x2, Pallas kernels, placed(): pl.pallas_call(place_kernel, out_shape=jax.ShapeDtypeStruct(shape, jnp.bf...  1.56 us
    pallas_call x1, Pallas kernels, per_device(): pl.pallas_call(right_kernel, out_shape=(jax.ShapeDtypeStruct((side, 5 * s...  1.36 us
  transfers between devices with their start and end apart: 7, of which 3 were waited for; matrix products, arithmetic and copies ran while one was open for 0% of the time, Pallas kernels for 21%

profile of v4, /device:TPU:0, one launch (start us, length us, event | category | flops | bytes accessed | tf_op | source)
XLA Modules:
  0.0 38.6 jit_solution(3834789913593172518)
XLA Ops:
  0.0 0.0 collective-permute-start
  0.0 8.2 %collective-permute-start.1 = (bf16[16,64,256]{2,1,0:T(8,128)(2,1)}, bf16[16,64,256]{2,1,0:T(8,128)(2,1)S(1)}, u32[]{:S(2)}, u32[]{:S(2)}) collective-permute-start(bf16[16,64,256]{2,1,0:T(8,128)(2,1)} %p_hbm.1), channel_id=1, source_target_pairs={{0,255},{1,0},{2,1},{3,2},{4,3},{5,4},{6,5},{7,6},{8,7},{9,8},{10,... | collective-permute-start | bytes 1572872 | tf_op jit(solution)/shard_map/ppermute | solution.py:17
  8.2 7.1 %left_kernel.1 = (bf16[3,384,1024]{2,1,0:T(8,128)(2,1)S(1)}, f32[384,384]{1,0:T(8,128)S(1)}, bf16[128,16,384]{2,1,0:T(8,128)(2,1)S(1)}) custom-call(s32[7,16]{1,0:T(8,128)} %bitcast.8, s32[4,4096]{1,0:T(4,128)} %bitcast.7, bf16[16,64,448]{2,1,0:T(8,128)(2,1)} %a_hbm.1, bf16[16,64,256]{2,1,0:T(8,128)(2,1)} %p_hbm.1), custom_call_target="tpu_custom_call" | custom-call | tf_op jit(solution)/shard_map/left_kernel/pallas_call | solution.py:229
  15.3 0.0 collective-permute-done.before_ref
  15.3 0.0 collective-permute-done.1.after_ref
  15.3 1.4 %right_kernel.1 = (bf16[128,640]{1,0:T(8,128)(2,1)S(1)}, f32[128,640]{1,0:T(8,128)S(1)}, bf16[128,640]{1,0:T(8,128)(2,1)S(1)}) custom-call(bf16[16,64,256]{2,1,0:T(8,128)(2,1)S(1)} %collective-permute-done.before_ref, bf16[16,64,256]{2,1,0:T(8,128)(2,1)S(1)} %collective-permute-done.1.after_ref, bf16[128,16,384]{2,1,0:T(8,128)(2,1)S(1)} %get-tuple-element.11.mask_ref, ...), custom_call_target="tpu_custom_call" | custom-call | tf_op jit(solution)/shard_map/right_kernel/pallas_call | solution.py:250
  16.7 0.1 collective-permute-start.2
  16.8 7.2 %collective-permute-start.3 = (bf16[128,640]{1,0:T(8,128)(2,1)S(1)}, bf16[128,640]{1,0:T(8,128)(2,1)S(1)}, u32[]{:S(2)}, u32[]{:S(2)}) collective-permute-start(bf16[128,640]{1,0:T(8,128)(2,1)S(1)} %get-tuple-element.16), channel_id=1, source_target_pairs={{0,255},{1,0},{2,1},{3,2},{4,3},{5,4},{6,5},{7,6},{8,7},{9,8},{10,... | collective-permute-start | bytes 491528 | tf_op jit(solution)/shard_map/ppermute | solution.py:17
  24.0 3.8 %collective-permute-done.2 = bf16[128,640]{1,0:T(8,128)(2,1)S(1)} collective-permute-done((bf16[128,640]{1,0:T(8,128)(2,1)S(1)}, bf16[128,640]{1,0:T(8,128)(2,1)S(1)}, u32[]{:S(2)}, u32[]{:S(2)}) %collective-permute-start.2) | collective-permute-done | bytes 163872 | tf_op jit(solution)/shard_map/ppermute | solution.py:17
  27.8 0.0 collective-permute-done.3
  27.8 0.1 collective-permute-start.5
  27.9 0.1 collective-permute-start.4
  28.0 2.0 %collective-permute-start.6 = (bf16[2,64,896]{2,1,0:T(8,128)(2,1)S(1)}, bf16[2,64,896]{2,1,0:T(8,128)(2,1)S(1)}, u32[]{:S(2)}, u32[]{:S(2)}) collective-permute-start(bf16[2,64,896]{2,1,0:T(8,128)(2,1)S(1)} %bitcast.5), channel_id=1, source_target_pairs={{0,64},{64,128},{128,192},{192,0},{1,65},{65,129},{129,193},{193,1... | collective-permute-start | bytes 688136 | tf_op jit(solution)/shard_map/ppermute | solution.py:17
  30.1 5.5 %collective-permute-done.5.refs_2_ = bf16[2,64,896]{2,1,0:T(8,128)(2,1)S(1)} collective-permute-done((bf16[2,64,896]{2,1,0:T(8,128)(2,1)S(1)}, bf16[2,64,896]{2,1,0:T(8,128)(2,1)S(1)}, u32[]{:S(2)}, u32[]{:S(2)}) %collective-permute-start.5) | collective-permute-done | bytes 229408 | tf_op jit(solution)/shard_map/ppermute | solution.py:17
  35.6 0.0 collective-permute-done.4.refs_1_
  35.6 0.9 %place_kernel.2.refs_0_ = bf16[8,64,896]{2,1,0:T(8,128)(2,1)} custom-call(bf16[2,64,896]{2,1,0:T(8,128)(2,1)S(1)} %bitcast.6, bf16[2,64,896]{2,1,0:T(8,128)(2,1)S(1)} %collective-permute-done.4.refs_1_, bf16[2,64,896]{2,1,0:T(8,128)(2,1)S(1)} %collective-permute-done.5.refs_2_), custom_call_target="tpu_custom_call" | custom-call | tf_op jit(solution)/shard_map/place_kernel/pallas_call | solution.py:195
  36.4 1.5 %collective-permute-done.6.refs_1_ = bf16[2,64,896]{2,1,0:T(8,128)(2,1)S(1)} collective-permute-done((bf16[2,64,896]{2,1,0:T(8,128)(2,1)S(1)}, bf16[2,64,896]{2,1,0:T(8,128)(2,1)S(1)}, u32[]{:S(2)}, u32[]{:S(2)}) %collective-permute-start.6) | collective-permute-done | bytes 229408 | tf_op jit(solution)/shard_map/ppermute | solution.py:17
  37.9 0.7 %place_kernel.3 = bf16[8,64,896]{2,1,0:T(8,128)(2,1)} custom-call(bf16[8,64,896]{2,1,0:T(8,128)(2,1)} %place_kernel.2.refs_0_, bf16[2,64,896]{2,1,0:T(8,128)(2,1)S(1)} %collective-permute-done.6.refs_1_), custom_call_target="tpu_custom_call", output_to_operand_aliasing={{}: (0, {})} | custom-call | tf_op jit(solution)/shard_map/place_kernel/pallas_call | solution.py:195
  (1 shorter events, 0.0 us)
Async XLA Ops:
  0.0 15.3 %collective-permute-start = (bf16[16,64,256]{2,1,0:T(8,128)(2,1)}, bf16[16,64,256]{2,1,0:T(8,128)(2,1)S(1)}, u32[]{:S(2)}, u32[]{:S(2)}) collective-permute-start(bf16[16,64,256]{2,1,0:T(8,128)(2,1)} %p_hbm.1), channel_id=1, source_target_pairs={{0,1},{1,2},{2,3},{3,4},{4,5},{5,6},{6,7},{7,8},{8,9},{9,10},{10,1... | collective-permute-start | bytes 1572872 | tf_op jit(solution)/shard_map/ppermute | solution.py:17
  0.0 15.3 %collective-permute-start.1 = (bf16[16,64,256]{2,1,0:T(8,128)(2,1)}, bf16[16,64,256]{2,1,0:T(8,128)(2,1)S(1)}, u32[]{:S(2)}, u32[]{:S(2)}) collective-permute-start(bf16[16,64,256]{2,1,0:T(8,128)(2,1)} %p_hbm.1), channel_id=1, source_target_pairs={{0,255},{1,0},{2,1},{3,2},{4,3},{5,4},{6,5},{7,6},{8,7},{9,8},{10,... | collective-permute-start | bytes 1572872 | tf_op jit(solution)/shard_map/ppermute | solution.py:17
  16.7 11.1 %collective-permute-start.2 = (bf16[128,640]{1,0:T(8,128)(2,1)S(1)}, bf16[128,640]{1,0:T(8,128)(2,1)S(1)}, u32[]{:S(2)}, u32[]{:S(2)}) collective-permute-start(bf16[128,640]{1,0:T(8,128)(2,1)S(1)} %get-tuple-element.14), channel_id=1, source_target_pairs={{0,1},{1,2},{2,3},{3,4},{4,5},{5,6},{6,7},{7,8},{8,9},{9,10},{10,1... | collective-permute-start | bytes 491528 | tf_op jit(solution)/shard_map/ppermute | solution.py:17
  16.8 11.0 %collective-permute-start.3 = (bf16[128,640]{1,0:T(8,128)(2,1)S(1)}, bf16[128,640]{1,0:T(8,128)(2,1)S(1)}, u32[]{:S(2)}, u32[]{:S(2)}) collective-permute-start(bf16[128,640]{1,0:T(8,128)(2,1)S(1)} %get-tuple-element.16), channel_id=1, source_target_pairs={{0,255},{1,0},{2,1},{3,2},{4,3},{5,4},{6,5},{7,6},{8,7},{9,8},{10,... | collective-permute-start | bytes 491528 | tf_op jit(solution)/shard_map/ppermute | solution.py:17
  27.8 7.7 %collective-permute-start.5 = (bf16[2,64,896]{2,1,0:T(8,128)(2,1)S(1)}, bf16[2,64,896]{2,1,0:T(8,128)(2,1)S(1)}, u32[]{:S(2)}, u32[]{:S(2)}) collective-permute-start(bf16[2,64,896]{2,1,0:T(8,128)(2,1)S(1)} %bitcast.3), channel_id=1, source_target_pairs={{0,128},{64,192},{128,0},{192,64},{1,129},{65,193},{129,1},{193,65... | collective-permute-start | bytes 688136 | tf_op jit(solution)/shard_map/ppermute | solution.py:17
  27.9 7.6 %collective-permute-start.4 = (bf16[2,64,896]{2,1,0:T(8,128)(2,1)S(1)}, bf16[2,64,896]{2,1,0:T(8,128)(2,1)S(1)}, u32[]{:S(2)}, u32[]{:S(2)}) collective-permute-start(bf16[2,64,896]{2,1,0:T(8,128)(2,1)S(1)} %bitcast.4), channel_id=1, source_target_pairs={{0,192},{64,0},{128,64},{192,128},{1,193},{65,1},{129,65},{193,129... | collective-permute-start | bytes 688136 | tf_op jit(solution)/shard_map/ppermute | solution.py:17
  28.0 9.9 %collective-permute-start.6 = (bf16[2,64,896]{2,1,0:T(8,128)(2,1)S(1)}, bf16[2,64,896]{2,1,0:T(8,128)(2,1)S(1)}, u32[]{:S(2)}, u32[]{:S(2)}) collective-permute-start(bf16[2,64,896]{2,1,0:T(8,128)(2,1)S(1)} %bitcast.5), channel_id=1, source_target_pairs={{0,64},{64,128},{128,192},{192,0},{1,65},{65,129},{129,193},{193,1... | collective-permute-start | bytes 688136 | tf_op jit(solution)/shard_map/ppermute | solution.py:17

commit v5 on v4

--- a/solution.py
+++ b/solution.py
@@ -8,6 +8,7 @@
 AGS = 8
 BS = 64
 LANES = 128
+CHUNK = 4
 VMEM_BYTES = 48 * 1024 * 1024
 BOTH = ("grp", "row")
 
@@ -61,12 +62,12 @@
                 ).astype(mask_ref.dtype)
 
 
-def dense_rows(blocks_ref, mask_ref, first):
-    rows, _, width = blocks_ref.shape
+def dense_rows(blocks_ref, mask_ref, first, start, count):
+    width = blocks_ref.shape[2]
     slots = width // BS
     packed = mask_ref.shape[1]
     parts = []
-    for row in range(rows):
+    for row in range(start, start + count):
         twice = []
         for pair in range(slots // 2):
             both = blocks_ref[row, :, pair * LANES : (pair + 1) * LANES]
@@ -149,8 +150,13 @@
     before_ref, after_ref, mask_ref, left_ref, own_ref, to_before_ref, stay_ref, to_after_ref
 ):
     def term(part, blocks_ref, first_mask):
-        dense = dense_rows(blocks_ref, mask_ref, first_mask)
-        return jnp.dot(left_ref[part], dense, preferred_element_type=jnp.float32)
+        total = None
+        for start in range(0, blocks_ref.shape[0], CHUNK):
+            dense = dense_rows(blocks_ref, mask_ref, first_mask, start, CHUNK)
+            inner = left_ref[part, :, start * BS : (start + CHUNK) * BS]
+            product = jnp.dot(inner, dense, preferred_element_type=jnp.float32)
+            total = product if total is None else total + product
+        return total
 
     first = term(0, before_ref, 0)
     last = term(2, after_ref, mask_ref.shape[0] // 2)

time: 38.7 us -> 38.7 us (level)
  no operation moved by 1% of the time
where the time goes in v5:
time: 38.7 us; the launch traced here: 38.6 us
  starting transfers between devices  17.7 us (46%)
  waiting for transfers between devices  10.8 us (28%)
  Pallas kernels  9.97 us (26%)
    ppermute x7, starting transfers between devices, shifted(): lax.ppermute(value, axis, [(i, (i + by) % peers) for i in range(peers)])  17.7 us
    ppermute x7, waiting for transfers between devices, shifted(): lax.ppermute(value, axis, [(i, (i + by) % peers) for i in range(peers)])  10.8 us
    pallas_call x1, Pallas kernels, per_device(): pl.pallas_call(left_kernel, out_shape=(jax.ShapeDtypeStruct((3, 3 * side,...  7.06 us
    pallas_call x2, Pallas kernels, placed(): pl.pallas_call(place_kernel, out_shape=jax.ShapeDtypeStruct(shape, jnp.bf...  1.56 us
    pallas_call x1, Pallas kernels, per_device(): pl.pallas_call(right_kernel, out_shape=(jax.ShapeDtypeStruct((side, 5 * s...  1.35 us
  transfers between devices with their start and end apart: 7, of which 3 were waited for; matrix products, arithmetic and copies ran while one was open for 0% of the time, Pallas kernels for 21%

profile of v5, /device:TPU:0, one launch (start us, length us, event | category | flops | bytes accessed | tf_op | source)
XLA Modules:
  0.0 38.6 jit_solution(13008504046572520894)
XLA Ops:
  0.0 0.0 collective-permute-start
  0.0 8.2 %collective-permute-start.1 = (bf16[16,64,256]{2,1,0:T(8,128)(2,1)}, bf16[16,64,256]{2,1,0:T(8,128)(2,1)S(1)}, u32[]{:S(2)}, u32[]{:S(2)}) collective-permute-start(bf16[16,64,256]{2,1,0:T(8,128)(2,1)} %p_hbm.1), channel_id=1, source_target_pairs={{0,255},{1,0},{2,1},{3,2},{4,3},{5,4},{6,5},{7,6},{8,7},{9,8},{10,... | collective-permute-start | bytes 1572872 | tf_op jit(solution)/shard_map/ppermute | solution.py:18
  8.2 7.1 %left_kernel.1 = (bf16[3,384,1024]{2,1,0:T(8,128)(2,1)S(1)}, f32[384,384]{1,0:T(8,128)S(1)}, bf16[128,16,384]{2,1,0:T(8,128)(2,1)S(1)}) custom-call(s32[7,16]{1,0:T(8,128)} %bitcast.8, s32[4,4096]{1,0:T(4,128)} %bitcast.7, bf16[16,64,448]{2,1,0:T(8,128)(2,1)} %a_hbm.1, bf16[16,64,256]{2,1,0:T(8,128)(2,1)} %p_hbm.1), custom_call_target="tpu_custom_call" | custom-call | tf_op jit(solution)/shard_map/left_kernel/pallas_call | solution.py:235
  15.3 0.0 collective-permute-done.before_ref
  15.3 0.0 collective-permute-done.1.after_ref
  15.3 1.3 %right_kernel.1 = (bf16[128,640]{1,0:T(8,128)(2,1)S(1)}, f32[128,640]{1,0:T(8,128)S(1)}, bf16[128,640]{1,0:T(8,128)(2,1)S(1)}) custom-call(bf16[16,64,256]{2,1,0:T(8,128)(2,1)S(1)} %collective-permute-done.before_ref, bf16[16,64,256]{2,1,0:T(8,128)(2,1)S(1)} %collective-permute-done.1.after_ref, bf16[128,16,384]{2,1,0:T(8,128)(2,1)S(1)} %get-tuple-element.11.mask_ref, ...), custom_call_target="tpu_custom_call" | custom-call | tf_op jit(solution)/shard_map/right_kernel/pallas_call | solution.py:256
  16.7 0.1 collective-permute-start.2
  16.7 7.2 %collective-permute-start.3 = (bf16[128,640]{1,0:T(8,128)(2,1)S(1)}, bf16[128,640]{1,0:T(8,128)(2,1)S(1)}, u32[]{:S(2)}, u32[]{:S(2)}) collective-permute-start(bf16[128,640]{1,0:T(8,128)(2,1)S(1)} %get-tuple-element.16), channel_id=1, source_target_pairs={{0,255},{1,0},{2,1},{3,2},{4,3},{5,4},{6,5},{7,6},{8,7},{9,8},{10,... | collective-permute-start | bytes 491528 | tf_op jit(solution)/shard_map/ppermute | solution.py:18
  24.0 3.8 %collective-permute-done.2 = bf16[128,640]{1,0:T(8,128)(2,1)S(1)} collective-permute-done((bf16[128,640]{1,0:T(8,128)(2,1)S(1)}, bf16[128,640]{1,0:T(8,128)(2,1)S(1)}, u32[]{:S(2)}, u32[]{:S(2)}) %collective-permute-start.2) | collective-permute-done | bytes 163872 | tf_op jit(solution)/shard_map/ppermute | solution.py:18
  27.8 0.0 collective-permute-done.3
  27.8 0.1 collective-permute-start.5
  27.9 0.1 collective-permute-start.4
  28.0 2.0 %collective-permute-start.6 = (bf16[2,64,896]{2,1,0:T(8,128)(2,1)S(1)}, bf16[2,64,896]{2,1,0:T(8,128)(2,1)S(1)}, u32[]{:S(2)}, u32[]{:S(2)}) collective-permute-start(bf16[2,64,896]{2,1,0:T(8,128)(2,1)S(1)} %bitcast.5), channel_id=1, source_target_pairs={{0,64},{64,128},{128,192},{192,0},{1,65},{65,129},{129,193},{193,1... | collective-permute-start | bytes 688136 | tf_op jit(solution)/shard_map/ppermute | solution.py:18
  30.1 5.5 %collective-permute-done.5.refs_2_ = bf16[2,64,896]{2,1,0:T(8,128)(2,1)S(1)} collective-permute-done((bf16[2,64,896]{2,1,0:T(8,128)(2,1)S(1)}, bf16[2,64,896]{2,1,0:T(8,128)(2,1)S(1)}, u32[]{:S(2)}, u32[]{:S(2)}) %collective-permute-start.5) | collective-permute-done | bytes 229408 | tf_op jit(solution)/shard_map/ppermute | solution.py:18
  35.6 0.0 collective-permute-done.4.refs_1_
  35.6 0.9 %place_kernel.2.refs_0_ = bf16[8,64,896]{2,1,0:T(8,128)(2,1)} custom-call(bf16[2,64,896]{2,1,0:T(8,128)(2,1)S(1)} %bitcast.6, bf16[2,64,896]{2,1,0:T(8,128)(2,1)S(1)} %collective-permute-done.4.refs_1_, bf16[2,64,896]{2,1,0:T(8,128)(2,1)S(1)} %collective-permute-done.5.refs_2_), custom_call_target="tpu_custom_call" | custom-call | tf_op jit(solution)/shard_map/place_kernel/pallas_call | solution.py:201
  36.4 1.5 %collective-permute-done.6.refs_1_ = bf16[2,64,896]{2,1,0:T(8,128)(2,1)S(1)} collective-permute-done((bf16[2,64,896]{2,1,0:T(8,128)(2,1)S(1)}, bf16[2,64,896]{2,1,0:T(8,128)(2,1)S(1)}, u32[]{:S(2)}, u32[]{:S(2)}) %collective-permute-start.6) | collective-permute-done | bytes 229408 | tf_op jit(solution)/shard_map/ppermute | solution.py:18
  37.9 0.7 %place_kernel.3 = bf16[8,64,896]{2,1,0:T(8,128)(2,1)} custom-call(bf16[8,64,896]{2,1,0:T(8,128)(2,1)} %place_kernel.2.refs_0_, bf16[2,64,896]{2,1,0:T(8,128)(2,1)S(1)} %collective-permute-done.6.refs_1_), custom_call_target="tpu_custom_call", output_to_operand_aliasing={{}: (0, {})} | custom-call | tf_op jit(solution)/shard_map/place_kernel/pallas_call | solution.py:201
  (1 shorter events, 0.0 us)
Async XLA Ops:
  0.0 15.3 %collective-permute-start = (bf16[16,64,256]{2,1,0:T(8,128)(2,1)}, bf16[16,64,256]{2,1,0:T(8,128)(2,1)S(1)}, u32[]{:S(2)}, u32[]{:S(2)}) collective-permute-start(bf16[16,64,256]{2,1,0:T(8,128)(2,1)} %p_hbm.1), channel_id=1, source_target_pairs={{0,1},{1,2},{2,3},{3,4},{4,5},{5,6},{6,7},{7,8},{8,9},{9,10},{10,1... | collective-permute-start | bytes 1572872 | tf_op jit(solution)/shard_map/ppermute | solution.py:18
  0.0 15.3 %collective-permute-start.1 = (bf16[16,64,256]{2,1,0:T(8,128)(2,1)}, bf16[16,64,256]{2,1,0:T(8,128)(2,1)S(1)}, u32[]{:S(2)}, u32[]{:S(2)}) collective-permute-start(bf16[16,64,256]{2,1,0:T(8,128)(2,1)} %p_hbm.1), channel_id=1, source_target_pairs={{0,255},{1,0},{2,1},{3,2},{4,3},{5,4},{6,5},{7,6},{8,7},{9,8},{10,... | collective-permute-start | bytes 1572872 | tf_op jit(solution)/shard_map/ppermute | solution.py:18
  16.7 11.1 %collective-permute-start.2 = (bf16[128,640]{1,0:T(8,128)(2,1)S(1)}, bf16[128,640]{1,0:T(8,128)(2,1)S(1)}, u32[]{:S(2)}, u32[]{:S(2)}) collective-permute-start(bf16[128,640]{1,0:T(8,128)(2,1)S(1)} %get-tuple-element.14), channel_id=1, source_target_pairs={{0,1},{1,2},{2,3},{3,4},{4,5},{5,6},{6,7},{7,8},{8,9},{9,10},{10,1... | collective-permute-start | bytes 491528 | tf_op jit(solution)/shard_map/ppermute | solution.py:18
  16.7 11.1 %collective-permute-start.3 = (bf16[128,640]{1,0:T(8,128)(2,1)S(1)}, bf16[128,640]{1,0:T(8,128)(2,1)S(1)}, u32[]{:S(2)}, u32[]{:S(2)}) collective-permute-start(bf16[128,640]{1,0:T(8,128)(2,1)S(1)} %get-tuple-element.16), channel_id=1, source_target_pairs={{0,255},{1,0},{2,1},{3,2},{4,3},{5,4},{6,5},{7,6},{8,7},{9,8},{10,... | collective-permute-start | bytes 491528 | tf_op jit(solution)/shard_map/ppermute | solution.py:18
  27.8 7.7 %collective-permute-start.5 = (bf16[2,64,896]{2,1,0:T(8,128)(2,1)S(1)}, bf16[2,64,896]{2,1,0:T(8,128)(2,1)S(1)}, u32[]{:S(2)}, u32[]{:S(2)}) collective-permute-start(bf16[2,64,896]{2,1,0:T(8,128)(2,1)S(1)} %bitcast.3), channel_id=1, source_target_pairs={{0,128},{64,192},{128,0},{192,64},{1,129},{65,193},{129,1},{193,65... | collective-permute-start | bytes 688136 | tf_op jit(solution)/shard_map/ppermute | solution.py:18
  27.9 7.6 %collective-permute-start.4 = (bf16[2,64,896]{2,1,0:T(8,128)(2,1)S(1)}, bf16[2,64,896]{2,1,0:T(8,128)(2,1)S(1)}, u32[]{:S(2)}, u32[]{:S(2)}) collective-permute-start(bf16[2,64,896]{2,1,0:T(8,128)(2,1)S(1)} %bitcast.4), channel_id=1, source_target_pairs={{0,192},{64,0},{128,64},{192,128},{1,193},{65,1},{129,65},{193,129... | collective-permute-start | bytes 688136 | tf_op jit(solution)/shard_map/ppermute | solution.py:18
  28.0 9.9 %collective-permute-start.6 = (bf16[2,64,896]{2,1,0:T(8,128)(2,1)S(1)}, bf16[2,64,896]{2,1,0:T(8,128)(2,1)S(1)}, u32[]{:S(2)}, u32[]{:S(2)}) collective-permute-start(bf16[2,64,896]{2,1,0:T(8,128)(2,1)S(1)} %bitcast.5), channel_id=1, source_target_pairs={{0,64},{64,128},{128,192},{192,0},{1,65},{65,129},{129,193},{193,1... | collective-permute-start | bytes 688136 | tf_op jit(solution)/shard_map/ppermute | solution.py:18
